TPU v7x, 1024 devices: a whole 4x8x16 slice. The times are simulated.
1024 devices in a mesh: wide: 64 (over y, x, core), narrow: 16 (over z).
Axes of the slice: x: 4, y: 8, z: 16, core: 2. Of those that a mesh axis runs over, the one named last changes fastest.
Arguments:
- gcm_state: float32 [8192, 144], P('wide'), may hold values from -6 to 6
- crm_state: bfloat16 [2, 60, 256, 8192], P(None, None, 'narrow', 'wide'), may hold values from -6 to 6
- courant: float32 [60, 8192], P(None, 'wide'), may hold values from 0.1 to 0.6
- cloud_mask: int32 [60, 8192], P(None, 'wide'), may hold values 0 or 1
- level_down: float32 [60, 72], replicated, may hold values from -0.75 to 0.75
- level_up: float32 [72, 60], replicated, may hold values from -0.75 to 0.75
- column_map: int32 [8192], replicated, may hold values from 0 to 8191, as said below
Outputs:
- gcm_tendency: bfloat16 [8192, 144], P('wide')
- crm_new: bfloat16 [2, 60, 256, 8192], P(None, None, 'narrow', 'wide')
Inputs may be any that keep to these rules, and one draw needn't show every extreme that they name: column_map is a bijection onto 0 to 8191; the columns of one index of wide go to at most 4 slots of any one owner, and to exactly 4 slots of half of the owners.
All inputs are finite; a program needn't handle non-finite values. No bound on the sum of `cloud_mask` on one device may be relied on, other than what follows from the above.
Results may differ from a plain program's by a relative error of at most 0.0048.
Values may be sent and summed in bfloat16 or wider, within the bound.
No kernel may reach another device: no remote copies, remote signals or barrier semaphores. Data moves between devices by JAX's collectives and lax.ppermute only.
A program may use at most 32 MiB of HBM per device.

v0:
```python
import jax
import jax.numpy as jnp
from jax import lax
from jax.sharding import PartitionSpec as P

CX = 256
SUB = 4


def with_halo(block, sides, width):
    for axis, dim in sides:
        count = lax.axis_size(axis)
        forward = [(i, i + 1) for i in range(count - 1)]
        forward.append((count - 1, 0))
        backward = [(target, source) for source, target in forward]
        low = lax.ppermute(
            lax.slice_in_dim(block, block.shape[dim] - width, None, axis=dim), axis, forward
        )
        high = lax.ppermute(lax.slice_in_dim(block, 0, width, axis=dim), axis, backward)
        block = jnp.concatenate([low, block, high], axis=dim)
    return block


def horizontal(padded, courant_now):
    left_cells = padded[:, :, :-2]
    middle = padded[:, :, 1:-1]
    right_cells = padded[:, :, 2:]
    return (
        middle
        + courant_now[None, :, None, :] * (left_cells - middle)
        + 0.15 * (right_cells - 2.0 * middle + left_cells)
    )


def column_physics(fields, forcing, cloudy):
    above_cells = jnp.concatenate([fields[:, 1:], fields[:, -1:]], axis=1)
    below_cells = jnp.concatenate([fields[:, :1], fields[:, :-1]], axis=1)
    fields = fields + 0.1 * (above_cells - 2.0 * fields + below_cells)
    fields = fields + 0.25 * forcing[:, :, None, :]
    moisture = fields[1]
    condensed = cloudy[:, None, :] * 0.3 * jnp.maximum(moisture, 0.0)
    return jnp.stack([fields[0] + 2.0 * condensed, moisture - condensed])


def shards(gcm_state, crm_state, courant, cloud_mask, level_down, level_up, column_map):
    wide_count = lax.axis_size("wide")
    wide_index = lax.axis_index("wide")
    columns = gcm_state.shape[0]
    capacity = 2 * columns // wide_count
    width_full = gcm_state.shape[1]
    levels = width_full // 2
    buffer_rows = wide_count * capacity
    my_targets = lax.dynamic_slice_in_dim(column_map, wide_index * columns, columns)
    my_owners = my_targets // columns
    position = jnp.arange(columns, dtype=jnp.int32)
    earlier = (my_owners[:, None] == my_owners[None, :]) & (position[None, :] < position[:, None])
    send_slot = my_owners * capacity + jnp.sum(earlier.astype(jnp.int32), axis=1)
    buffer_index = jnp.arange(buffer_rows, dtype=jnp.int32)
    send_match = (send_slot[None, :] == buffer_index[:, None]).astype(jnp.int32)
    send_filled = jnp.sum(send_match, axis=1) > 0
    send_source = jnp.sum(send_match * position[None, :], axis=1)
    all_targets = column_map.reshape(wide_count, columns)
    is_mine = all_targets // columns == wide_index
    rank_mine = jnp.cumsum(is_mine.astype(jnp.int32), axis=1) - 1
    local_slot = all_targets % columns
    within_cap = jnp.arange(capacity, dtype=jnp.int32)
    arrive_match = (
        is_mine[:, None, :] & (rank_mine[:, None, :] == within_cap[None, :, None])
    ).astype(jnp.int32)
    slot_of_buffer = jnp.sum(arrive_match * local_slot[:, None, :], axis=2).reshape(buffer_rows)
    arrive_filled = (jnp.sum(arrive_match, axis=2) > 0).reshape(buffer_rows)
    slot_match = (arrive_filled[:, None] & (slot_of_buffer[:, None] == position[None, :])).astype(
        jnp.int32
    )
    buffer_of_slot = jnp.sum(slot_match * buffer_index[:, None], axis=0)
    outgoing = gcm_state.astype(jnp.bfloat16)
    packed = jnp.where(send_filled[:, None], outgoing[send_source], jnp.zeros((), jnp.bfloat16))
    arrived = lax.all_to_all(packed, "wide", split_axis=0, concat_axis=0, tiled=True)
    slot_rows = arrived[buffer_of_slot].astype(jnp.float32).reshape(columns, 2, levels)
    forcing = jnp.einsum("sfm,lm->fls", slot_rows, level_down, precision=lax.Precision.HIGHEST)
    cloudy = cloud_mask.astype(jnp.float32)
    initial = crm_state.astype(jnp.float32)
    fields = initial
    for substep in range(SUB):
        padded = with_halo(fields, (("narrow", 2),), 1)
        fields = column_physics(horizontal(padded, courant), forcing, cloudy)
    crm_new = fields.astype(jnp.bfloat16)
    diff_sums = jnp.sum(fields - initial, axis=2)
    partial_term = jnp.einsum(
        "fls,ml->sfm", diff_sums, level_up, precision=lax.Precision.HIGHEST
    ) * (1.0 / (CX * SUB))
    partial_term = partial_term.reshape(columns, width_full)
    totals = lax.psum(partial_term, "narrow").astype(jnp.bfloat16)
    returned = lax.all_to_all(
        totals[slot_of_buffer], "wide", split_axis=0, concat_axis=0, tiled=True
    )
    gcm_tendency = returned[send_slot]
    return (gcm_tendency, crm_new)


def solution(mesh):
    placed = (
        P("wide", None),
        P(None, None, "narrow", "wide"),
        P(None, "wide"),
        P(None, "wide"),
        P(),
        P(),
        P(),
    )
    return jax.shard_map(
        shards,
        mesh=mesh,
        in_specs=placed,
        out_specs=(P("wide", None), P(None, None, "narrow", "wide")),
        check_vma=False,
    )
```

profile of v0, /device:TPU:1, one launch (start us, length us, event | category | flops | bytes accessed | tf_op | source)
XLA Modules:
  0.0 159.0 jit_solution(17328320254864746075)
XLA Ops:
  0.7 0.8 and_select_fusion
  1.6 0.8 compare_select_fusion.2
  2.7 0.9 convert_element_type.36
  3.7 1.2 gather_fusion
  4.9 0.8 broadcast_select_fusion
  5.7 18.2 %all-to-all-start = ((bf16[64,4,144]{2,1,0:T(4,128)(2,1)}), bf16[64,4,144]{2,1,0:T(4,128)(2,1)S(1)}, u32[]{:S(2)}, u32[]{:S(2)}) async-start(bf16[64,4,144]{2,1,0:T(4,128)(2,1)} %broadcast_select_fusion), calls=%async_computation | async-start | bytes 262144 | tf_op jit(solution)/shard_map/all_to_all | solution.py:78
  24.0 1.9 %collective-permute-start = (f32[2,60,1,128]{3,2,1,0:T(1,128)S(1)}, f32[2,60,1,128]{3,2,1,0:T(1,128)S(1)}, u32[]{:S(2)}, u32[]{:S(2)}) collective-permute-start(f32[2,60,1,128]{3,2,1,0:T(1,128)S(1)} %get-tuple-element.48), channel_id=1, source_target_pairs={{0,1},{1,2},{2,3},{3,4},{4,5},{5,6},{6,7},{7,8},{8,9},{9,10},{10,1... | collective-permute-start | bytes 184328 | tf_op jit(solution)/shard_map/ppermute | solution.py:16
  25.9 11.4 %collective-permute-start.1 = (f32[2,60,1,128]{3,2,1,0:T(1,128)S(1)}, f32[2,60,1,128]{3,2,1,0:T(1,128)S(1)}, u32[]{:S(2)}, u32[]{:S(2)}) collective-permute-start(f32[2,60,1,128]{3,2,1,0:T(1,128)S(1)} %get-tuple-element.49), channel_id=1, source_target_pairs={{1,0},{2,1},{3,2},{4,3},{5,4},{6,5},{7,6},{8,7},{9,8},{10,9},{11,1... | collective-permute-start | bytes 184328 | tf_op jit(solution)/shard_map/ppermute | solution.py:19
  37.5 0.7 copy-done.5
  40.4 0.8 gather_fusion.1
  42.2 0.7 fusion.35
  43.1 1.9 %collective-permute-start.2 = (f32[2,60,1,128]{3,2,1,0:T(1,128)S(1)}, f32[2,60,1,128]{3,2,1,0:T(1,128)S(1)}, u32[]{:S(2)}, u32[]{:S(2)}) collective-permute-start(f32[2,60,1,128]{3,2,1,0:T(1,128)S(1)} %get-tuple-element.42), channel_id=1, source_target_pairs={{0,1},{1,2},{2,3},{3,4},{4,5},{5,6},{6,7},{7,8},{8,9},{9,10},{10,1... | collective-permute-start | bytes 184328 | tf_op jit(solution)/shard_map/ppermute | solution.py:16
  45.1 6.0 %collective-permute-start.3 = (f32[2,60,1,128]{3,2,1,0:T(1,128)S(1)}, f32[2,60,1,128]{3,2,1,0:T(1,128)S(1)}, u32[]{:S(2)}, u32[]{:S(2)}) collective-permute-start(f32[2,60,1,128]{3,2,1,0:T(1,128)S(1)} %get-tuple-element.43), channel_id=1, source_target_pairs={{1,0},{2,1},{3,2},{4,3},{5,4},{6,5},{7,6},{8,7},{9,8},{10,9},{11,1... | collective-permute-start | bytes 184328 | tf_op jit(solution)/shard_map/ppermute | solution.py:19
  51.2 1.2 collective-permute-done.3
  53.0 0.7 fusion.39
  53.9 1.9 %collective-permute-start.4 = (f32[2,60,1,128]{3,2,1,0:T(1,128)S(1)}, f32[2,60,1,128]{3,2,1,0:T(1,128)S(1)}, u32[]{:S(2)}, u32[]{:S(2)}) collective-permute-start(f32[2,60,1,128]{3,2,1,0:T(1,128)S(1)} %get-tuple-element.36), channel_id=1, source_target_pairs={{0,1},{1,2},{2,3},{3,4},{4,5},{5,6},{6,7},{7,8},{8,9},{9,10},{10,1... | collective-permute-start | bytes 184328 | tf_op jit(solution)/shard_map/ppermute | solution.py:16
  55.9 4.9 %collective-permute-start.5 = (f32[2,60,1,128]{3,2,1,0:T(1,128)S(1)}, f32[2,60,1,128]{3,2,1,0:T(1,128)S(1)}, u32[]{:S(2)}, u32[]{:S(2)}) collective-permute-start(f32[2,60,1,128]{3,2,1,0:T(1,128)S(1)} %get-tuple-element.37), channel_id=1, source_target_pairs={{1,0},{2,1},{3,2},{4,3},{5,4},{6,5},{7,6},{8,7},{9,8},{10,9},{11,1... | collective-permute-start | bytes 184328 | tf_op jit(solution)/shard_map/ppermute | solution.py:19
  60.8 1.2 collective-permute-done.5
  62.7 0.7 fusion.43
  63.7 1.9 %collective-permute-start.6 = (f32[2,60,1,128]{3,2,1,0:T(1,128)S(1)}, f32[2,60,1,128]{3,2,1,0:T(1,128)S(1)}, u32[]{:S(2)}, u32[]{:S(2)}) collective-permute-start(f32[2,60,1,128]{3,2,1,0:T(1,128)S(1)} %get-tuple-element.30), channel_id=1, source_target_pairs={{0,1},{1,2},{2,3},{3,4},{4,5},{5,6},{6,7},{7,8},{8,9},{9,10},{10,1... | collective-permute-start | bytes 184328 | tf_op jit(solution)/shard_map/ppermute | solution.py:16
  65.6 4.9 %collective-permute-start.7 = (f32[2,60,1,128]{3,2,1,0:T(1,128)S(1)}, f32[2,60,1,128]{3,2,1,0:T(1,128)S(1)}, u32[]{:S(2)}, u32[]{:S(2)}) collective-permute-start(f32[2,60,1,128]{3,2,1,0:T(1,128)S(1)} %get-tuple-element.31), channel_id=1, source_target_pairs={{1,0},{2,1},{3,2},{4,3},{5,4},{6,5},{7,6},{8,7},{9,8},{10,9},{11,1... | collective-permute-start | bytes 184328 | tf_op jit(solution)/shard_map/ppermute | solution.py:19
  70.5 1.2 collective-permute-done.7
  72.5 0.7 fusion.47
  73.3 0.9 copy-done.2
  74.9 42.8 %psum.7 = bf16[128,144]{1,0:T(8,128)(2,1)S(1)} all-reduce(f32[128,144]{1,0:T(8,128)S(1)} %copy.28), channel_id=1, replica_groups=mesh['wide'=64,'narrow'=16] {'narrow'}, use_global_device_ids=true, to_apply=%region_8.9 | all-reduce | flops 18432 | bytes 110592 | tf_op jit(solution)/shard_map/psum | solution.py:93
  117.6 1.2 gather_fusion.2
  118.8 0.7 all_to_all.16
  119.5 26.7 %all-to-all-start.1 = ((bf16[64,4,144]{2,1,0:T(4,128)(2,1)}), bf16[64,4,144]{2,1,0:T(4,128)(2,1)S(1)}, u32[]{:S(2)}, u32[]{:S(2)}) async-start(bf16[64,4,144]{2,1,0:T(4,128)(2,1)} %all_to_all.16), calls=%async_computation.1 | async-start | bytes 262144 | tf_op jit(solution)/shard_map/all_to_all | solution.py:94
  146.3 0.8 fusion.48
  147.1 10.2 %all-to-all-done.1 = bf16[64,4,144]{2,1,0:T(4,128)(2,1)S(1)} async-done(((bf16[64,4,144]{2,1,0:T(4,128)(2,1)}), bf16[64,4,144]{2,1,0:T(4,128)(2,1)S(1)}, u32[]{:S(2)}, u32[]{:S(2)}) %all-to-all-start.1) | async-done | bytes 73760 | tf_op jit(solution)/shard_map/all_to_all | solution.py:94
  157.4 0.8 gather_fusion.3
  158.3 0.7 copy.30
  (71 shorter events, 7.5 us)
Async XLA Ops:
  0.6 73.9 %copy-start = (f32[72,60]{0,1:T(8,128)S(1)}, f32[72,60]{0,1:T(8,128)}, u32[]{:S(2)}) copy-start(f32[72,60]{0,1:T(8,128)} %param.12) | copy-start | bytes 51844
  4.8 19.0 %copy-start.1 = (bf16[2,60,16,128]{3,2,1,0:T(8,128)(2,1)S(1)}, bf16[2,60,16,128]{3,2,1,0:T(8,128)(2,1)}, u32[]{:S(2)}) copy-start(bf16[2,60,16,128]{3,2,1,0:T(8,128)(2,1)} %param.8) | copy-start | bytes 1474564
  5.7 34.6 %all-to-all-start = ((bf16[64,4,144]{2,1,0:T(4,128)(2,1)}), bf16[64,4,144]{2,1,0:T(4,128)(2,1)S(1)}, u32[]{:S(2)}, u32[]{:S(2)}) async-start(bf16[64,4,144]{2,1,0:T(4,128)(2,1)} %broadcast_select_fusion), calls=%async_computation | async-start | bytes 262144 | tf_op jit(solution)/shard_map/all_to_all | solution.py:78
  23.9 13.4 %copy-start.4 = (s32[8192]{0:T(1024)S(1)}, s32[8192]{0:T(1024)}, u32[]{:S(2)}) copy-start(s32[8192]{0:T(1024)} %param.13) | copy-start | bytes 98308
  24.0 15.3 %collective-permute-start = (f32[2,60,1,128]{3,2,1,0:T(1,128)S(1)}, f32[2,60,1,128]{3,2,1,0:T(1,128)S(1)}, u32[]{:S(2)}, u32[]{:S(2)}) collective-permute-start(f32[2,60,1,128]{3,2,1,0:T(1,128)S(1)} %get-tuple-element.48), channel_id=1, source_target_pairs={{0,1},{1,2},{2,3},{3,4},{4,5},{5,6},{6,7},{7,8},{8,9},{9,10},{10,1... | collective-permute-start | bytes 184328 | tf_op jit(solution)/shard_map/ppermute | solution.py:16
  25.9 13.4 %collective-permute-start.1 = (f32[2,60,1,128]{3,2,1,0:T(1,128)S(1)}, f32[2,60,1,128]{3,2,1,0:T(1,128)S(1)}, u32[]{:S(2)}, u32[]{:S(2)}) collective-permute-start(f32[2,60,1,128]{3,2,1,0:T(1,128)S(1)} %get-tuple-element.49), channel_id=1, source_target_pairs={{1,0},{2,1},{3,2},{4,3},{5,4},{6,5},{7,6},{8,7},{9,8},{10,9},{11,1... | collective-permute-start | bytes 184328 | tf_op jit(solution)/shard_map/ppermute | solution.py:19
  37.4 0.8 copy-start.5
  38.9 0.8 copy-start.3
  41.3 0.8 copy-start.6
  43.1 8.1 %collective-permute-start.2 = (f32[2,60,1,128]{3,2,1,0:T(1,128)S(1)}, f32[2,60,1,128]{3,2,1,0:T(1,128)S(1)}, u32[]{:S(2)}, u32[]{:S(2)}) collective-permute-start(f32[2,60,1,128]{3,2,1,0:T(1,128)S(1)} %get-tuple-element.42), channel_id=1, source_target_pairs={{0,1},{1,2},{2,3},{3,4},{4,5},{5,6},{6,7},{7,8},{8,9},{9,10},{10,1... | collective-permute-start | bytes 184328 | tf_op jit(solution)/shard_map/ppermute | solution.py:16
  45.1 7.3 %collective-permute-start.3 = (f32[2,60,1,128]{3,2,1,0:T(1,128)S(1)}, f32[2,60,1,128]{3,2,1,0:T(1,128)S(1)}, u32[]{:S(2)}, u32[]{:S(2)}) collective-permute-start(f32[2,60,1,128]{3,2,1,0:T(1,128)S(1)} %get-tuple-element.43), channel_id=1, source_target_pairs={{1,0},{2,1},{3,2},{4,3},{5,4},{6,5},{7,6},{8,7},{9,8},{10,9},{11,1... | collective-permute-start | bytes 184328 | tf_op jit(solution)/shard_map/ppermute | solution.py:19
  53.9 6.8 %collective-permute-start.4 = (f32[2,60,1,128]{3,2,1,0:T(1,128)S(1)}, f32[2,60,1,128]{3,2,1,0:T(1,128)S(1)}, u32[]{:S(2)}, u32[]{:S(2)}) collective-permute-start(f32[2,60,1,128]{3,2,1,0:T(1,128)S(1)} %get-tuple-element.36), channel_id=1, source_target_pairs={{0,1},{1,2},{2,3},{3,4},{4,5},{5,6},{6,7},{7,8},{8,9},{9,10},{10,1... | collective-permute-start | bytes 184328 | tf_op jit(solution)/shard_map/ppermute | solution.py:16
  55.9 6.2 %collective-permute-start.5 = (f32[2,60,1,128]{3,2,1,0:T(1,128)S(1)}, f32[2,60,1,128]{3,2,1,0:T(1,128)S(1)}, u32[]{:S(2)}, u32[]{:S(2)}) collective-permute-start(f32[2,60,1,128]{3,2,1,0:T(1,128)S(1)} %get-tuple-element.37), channel_id=1, source_target_pairs={{1,0},{2,1},{3,2},{4,3},{5,4},{6,5},{7,6},{8,7},{9,8},{10,9},{11,1... | collective-permute-start | bytes 184328 | tf_op jit(solution)/shard_map/ppermute | solution.py:19
  63.7 6.8 %collective-permute-start.6 = (f32[2,60,1,128]{3,2,1,0:T(1,128)S(1)}, f32[2,60,1,128]{3,2,1,0:T(1,128)S(1)}, u32[]{:S(2)}, u32[]{:S(2)}) collective-permute-start(f32[2,60,1,128]{3,2,1,0:T(1,128)S(1)} %get-tuple-element.30), channel_id=1, source_target_pairs={{0,1},{1,2},{2,3},{3,4},{4,5},{5,6},{6,7},{7,8},{8,9},{9,10},{10,1... | collective-permute-start | bytes 184328 | tf_op jit(solution)/shard_map/ppermute | solution.py:16
  65.6 6.2 %collective-permute-start.7 = (f32[2,60,1,128]{3,2,1,0:T(1,128)S(1)}, f32[2,60,1,128]{3,2,1,0:T(1,128)S(1)}, u32[]{:S(2)}, u32[]{:S(2)}) collective-permute-start(f32[2,60,1,128]{3,2,1,0:T(1,128)S(1)} %get-tuple-element.31), channel_id=1, source_target_pairs={{1,0},{2,1},{3,2},{4,3},{5,4},{6,5},{7,6},{8,7},{9,8},{10,9},{11,1... | collective-permute-start | bytes 184328 | tf_op jit(solution)/shard_map/ppermute | solution.py:19
  73.2 1.0 copy-start.2
  119.5 37.8 %all-to-all-start.1 = ((bf16[64,4,144]{2,1,0:T(4,128)(2,1)}), bf16[64,4,144]{2,1,0:T(4,128)(2,1)S(1)}, u32[]{:S(2)}, u32[]{:S(2)}) async-start(bf16[64,4,144]{2,1,0:T(4,128)(2,1)} %all_to_all.16), calls=%async_computation.1 | async-start | bytes 262144 | tf_op jit(solution)/shard_map/all_to_all | solution.py:94
where the time goes:
time: 160 us; the launch traced here: 159 us
  starting transfers between devices  79.8 us (50%)
  blocking collectives  42.8 us (27%)
  waiting for transfers between devices  13.9 us (9%)
  other arithmetic  11.1 us (7%)
  local copies, waits for them, and re-layouts  9.89 us (6%)
    psum x1, blocking collectives, shards(): totals = lax.psum(partial_term, 'narrow').astype(jnp.bfloat16)  42.8 us
    ppermute x4, starting transfers between devices, with_halo(): lax.ppermute(lax.slice_in_dim(block, 0, width, axis=dim), axis, backward)  27.2 us
    all_to_all x1, starting transfers between devices, shards(): lax.all_to_all(totals[slot_of_buffer], 'wide', split_axis=0, concat_axis=...  26.7 us
    all_to_all x1, starting transfers between devices, shards(): lax.all_to_all(packed, 'wide', split_axis=0, concat_axis=0, tiled=True)  18.2 us
    all_to_all x1, waiting for transfers between devices, shards(): lax.all_to_all(totals[slot_of_buffer], 'wide', split_axis=0, concat_axis=...  10.2 us
    ppermute x4, starting transfers between devices, with_halo(): lax.ppermute(lax.slice_in_dim(block, block.shape[dim] - width, None, axis...  7.68 us
    ppermute x4, waiting for transfers between devices, with_halo(): lax.ppermute(lax.slice_in_dim(block, 0, width, axis=dim), axis, backward)  3.66 us
    unnamed x15, local copies, waits for them, and re-layouts  3.32 us
  transfers between devices with their start and end apart: 10, of which 4 were waited for; matrix products, arithmetic and copies ran while one was open for 2% of the time, Pallas kernels for 0%

commit v1 on v0

v1 whole, which is shorter than its diff:
```python
import functools

import jax
import jax.numpy as jnp
from jax import lax
from jax.experimental import pallas as pl
from jax.experimental.pallas import tpu as pltpu
from jax.sharding import PartitionSpec as P

CX = 256
SUB = 4
CAP = 4
ROWS = 6
LANES = 128
EXTRA = 16
HI = lax.Precision.HIGHEST
F32 = jnp.float32
BF16 = jnp.bfloat16


def iota(shape, dim):
    return lax.broadcasted_iota(jnp.int32, shape, dim)


def dot(a, b, dims):
    return lax.dot_general(a, b, (dims, ((), ())), preferred_element_type=F32)


def split3(x):
    a = x.astype(BF16)
    r = x - a.astype(F32)
    b = r.astype(BF16)
    c = (r - b.astype(F32)).astype(BF16)
    return a, b, c


def row_parts(n):
    row = iota((n, LANES), 0)
    peer = (row * 10923) >> 16
    return peer, row - peer * ROWS


def before_matrix():
    return (iota((LANES, LANES), 0) < iota((LANES, LANES), 1)).astype(BF16)


def pack_kernel(w_ref, map_ref, state_ref, wire_ref, owner_ref, rank_ref):
    peers = map_ref.shape[0]
    mine = map_ref[pl.ds(w_ref[0], 1), :] >> 7
    own = iota((peers, LANES), 0) == mine
    own_b = own.astype(BF16)
    count = dot(own_b, before_matrix(), ((1,), (0,)))
    rank = jnp.sum(jnp.where(own, count, 0.0), axis=0, keepdims=True).astype(jnp.int32)
    owner_ref[...] = own_b
    rank_ref[...] = jnp.broadcast_to(rank, rank_ref.shape)
    n = peers * ROWS
    peer, part = row_parts(n)
    to_peer = peer == mine
    main = (to_peer & (part == rank)).astype(BF16)
    tail = (to_peer & (part == CAP)).astype(BF16)
    state = state_ref[...].astype(BF16)
    levels = state.shape[0]
    extra = state[LANES:levels].astype(F32)
    spread = [jnp.where(rank == k, extra, 0.0) for k in range(CAP)]
    spread.append(jnp.zeros((LANES - CAP * EXTRA, LANES), F32))
    spread = jnp.concatenate(spread, axis=0).astype(BF16)
    wire = dot(main, state[:LANES], ((1,), (1,))) + dot(tail, spread, ((1,), (1,)))
    wire_ref[...] = wire.astype(BF16)


def route_kernel(w_ref, map_ref, slot_ref, take_ref, rank_ref):
    peers = map_ref.shape[0]
    targets = map_ref[...]
    here = (targets >> 7) == w_ref[0]
    local = (targets & (LANES - 1)).astype(F32) + 1.0
    count = dot(here.astype(BF16), before_matrix(), ((1,), (0,)))
    slots = []
    lane = iota((peers, LANES), 1).astype(F32) + 1.0
    for k in range(CAP):
        hit = here & (count == float(k))
        one = jnp.sum(jnp.where(hit, local, 0.0), axis=1, keepdims=True)
        slots.append((one == lane).astype(F32))
    rank = jnp.zeros((1, LANES), F32)
    anyslot = jnp.zeros((peers, LANES), F32)
    for k in range(CAP):
        rank = rank + float(k) * jnp.sum(slots[k], axis=0, keepdims=True)
        anyslot = anyslot + slots[k]
        slot_ref[:, k * LANES : (k + 1) * LANES] = slots[k].astype(BF16)
    rank_ref[...] = jnp.broadcast_to(rank, rank_ref.shape).astype(jnp.int32)
    n = peers * ROWS
    row = iota((n, peers), 0)
    peer = (row * 10923) >> 16
    part = row - peer * ROWS
    same = peer == iota((n, peers), 1)
    main = jnp.zeros((n, LANES), F32)
    for k in range(CAP):
        main = main + dot((same & (part == k)).astype(BF16), slots[k].astype(BF16), ((1,), (0,)))
    tail = dot((same & (part == CAP)).astype(BF16), anyslot.astype(BF16), ((1,), (0,)))
    take_ref[:, :LANES] = main.astype(BF16)
    take_ref[:, LANES:] = tail.astype(BF16)


def horizontal(x, a0, a1, keep=None):
    n = x.shape[0]
    left = pltpu.roll(x, 1, 0)
    right = pltpu.roll(x, n - 1, 0)
    if keep is not None:
        left, x, right = left[:keep], x[:keep], right[:keep]
    return a1 * left + a0 * x + 0.15 * right


def start_kernel(crm_ref, low_ref, high_ref, courant_ref, out_ref):
    levels = crm_ref.shape[1]

    def mixed(level):
        c = courant_ref[pl.ds(level, 1), :]
        a0, a1 = 0.7 - c, c + 0.15
        result = []
        for f in range(2):
            x = jnp.concatenate(
                [
                    crm_ref[f, level].astype(F32),
                    high_ref[f, level].astype(F32),
                    low_ref[f, level].astype(F32),
                ],
                axis=0,
            )
            result.append(horizontal(x, a0, a1))
        return tuple(result)

    def body(level, carry):
        below, here = carry
        above = mixed(jnp.minimum(level + 1, levels - 1))
        for f in range(2):
            out_ref[f, level] = 0.8 * here[f] + 0.1 * (above[f] + below[f])
        return here, above

    first = mixed(0)
    lax.fori_loop(0, levels, body, (first, first), unroll=4)


def main_kernel(
    wire_ref, take_ref, rank_ref, start_ref, crm_ref, courant_ref, mask_ref, down_ref,
    new_ref, diff_ref, force_ref, cloud_ref, field_ref,
):
    levels = crm_ref.shape[1]
    gcm = down_ref.shape[1]
    own = crm_ref.shape[2]
    got = dot(wire_ref[...], take_ref[...], ((0,), (0,)))
    tail = jnp.zeros((EXTRA, LANES), F32)
    rank = rank_ref[0:1, :]
    for k in range(CAP):
        tail = tail + jnp.where(rank == k, got[k * EXTRA : (k + 1) * EXTRA, LANES:], 0.0)
    rows = jnp.concatenate([got[:, :LANES], tail], axis=0)
    for f in range(2):
        force = lax.dot_general(
            down_ref[...], rows[f * gcm : (f + 1) * gcm], (((1,), (0,)), ((), ())),
            precision=HI, preferred_element_type=F32,
        )
        force_ref[f, :levels] = 0.25 * force
    cloud_ref[...] = mask_ref[...].astype(F32) * 0.3
    diff_ref[...] = jnp.zeros_like(diff_ref)

    def physics(pair, level):
        t = pair[0] + force_ref[0, pl.ds(level, 1), :]
        q = pair[1] + force_ref[1, pl.ds(level, 1), :]
        condensed = cloud_ref[pl.ds(level, 1), :] * jnp.maximum(q, 0.0)
        return t + 2.0 * condensed, q - condensed

    def substep(index):
        source = start_ref if index == 1 else field_ref
        last = index == SUB - 1
        keep = own if last else None

        def mixed(level):
            c = courant_ref[pl.ds(level, 1), :]
            a0, a1 = 0.7 - c, c + 0.15
            pair = (source[0, level], source[1, level])
            if index == 1:
                pair = physics(pair, level)
            return tuple(horizontal(x, a0, a1, keep) for x in pair)

        def body(level, carry):
            below, here = carry
            above = mixed(jnp.minimum(level + 1, levels - 1))
            pair = tuple(0.8 * here[f] + 0.1 * (above[f] + below[f]) for f in range(2))
            pair = physics(pair, level)
            for f in range(2):
                if last:
                    new_ref[f, level] = pair[f].astype(BF16)
                    change = pair[f] - crm_ref[f, level].astype(F32)
                    diff_ref[f, pl.ds(level, 1), :] = jnp.sum(change, axis=0, keepdims=True)
                else:
                    field_ref[f, level] = pair[f]
            return here, above

        first = mixed(0)
        lax.fori_loop(0, levels, body, (first, first), unroll=4)

    for index in range(1, SUB):
        substep(index)


def turn_kernel(part_ref, slot_ref, wire_ref):
    total = jnp.sum(part_ref[...], axis=0)
    peers = wire_ref.shape[0]
    rows = total.shape[0]
    wire = jnp.zeros((peers, LANES), F32)
    for piece in split3(total):
        for k in range(CAP):
            padded = []
            if k:
                padded.append(jnp.zeros((k * rows, LANES), F32))
            padded.append(piece.astype(F32))
            padded.append(jnp.zeros((LANES - (k + 1) * rows, LANES), F32))
            block = jnp.concatenate(padded, axis=0).astype(BF16)
            wire = wire + dot(slot_ref[:, k * LANES : (k + 1) * LANES], block, ((1,), (1,)))
    wire_ref[...] = wire


def back_kernel(wire_ref, owner_ref, rank_ref, out_ref):
    rows = out_ref.shape[1]
    got = jnp.zeros((LANES, LANES), F32)
    for piece in split3(wire_ref[...]):
        got = got + dot(piece, owner_ref[...], ((0,), (0,)))
    rank = rank_ref[0:1, :]
    change = jnp.zeros((rows, LANES), F32)
    for k in range(CAP):
        change = change + jnp.where(rank == k, got[k * rows : (k + 1) * rows], 0.0)
    out_ref[...] = jnp.broadcast_to(change[None], out_ref.shape)


def end_kernel(change_ref, up_ref, out_ref):
    levels, gcm = up_ref.shape
    half = change_ref.shape[0] // 2
    for f in range(2):
        tend = lax.dot_general(
            up_ref[...], change_ref[f * half : f * half + levels], (((0,), (0,)), ((), ())),
            precision=HI, preferred_element_type=F32,
        ) * (1.0 / (CX * SUB))
        out_ref[f * gcm : (f + 1) * gcm] = tend.astype(BF16)


VM = pl.BlockSpec(memory_space=pltpu.VMEM)
SM = pl.BlockSpec(memory_space=pltpu.SMEM)


def call(kernel, shapes, specs, *args, scratch=()):
    out = [jax.ShapeDtypeStruct(s, d) for s, d in shapes]
    many = len(out) > 1
    return pl.pallas_call(
        kernel,
        out_shape=out if many else out[0],
        in_specs=specs,
        out_specs=[VM] * len(out) if many else VM,
        scratch_shapes=list(scratch),
    )(*args)


def shards(gcm_state, crm_state, courant, cloud_mask, level_down, level_up, column_map):
    peers = lax.axis_size("wide")
    ring = lax.axis_size("narrow")
    columns, width = gcm_state.shape
    levels = crm_state.shape[1]
    own = crm_state.shape[2]
    w = lax.axis_index("wide").astype(jnp.int32).reshape(1)
    targets = column_map.reshape(peers, columns)
    n = peers * ROWS

    wire, owner, send_rank = call(
        pack_kernel,
        [((n, LANES), BF16), ((peers, LANES), BF16), ((8, LANES), jnp.int32)],
        [SM, VM, VM], w, targets, gcm_state.T,
    )
    arrived = lax.all_to_all(
        wire.reshape(n // 2, 2, LANES), "wide", split_axis=0, concat_axis=0, tiled=True
    ).reshape(n, LANES)

    forward = [(i, (i + 1) % ring) for i in range(ring)]
    backward = [(b, a) for a, b in forward]
    low = lax.ppermute(crm_state[:, :, own - SUB :], "narrow", forward)
    high = lax.ppermute(crm_state[:, :, :SUB], "narrow", backward)

    slots, take, take_rank = call(
        route_kernel,
        [((peers, CAP * LANES), BF16), ((n, 2 * LANES), BF16), ((8, LANES), jnp.int32)],
        [SM, VM], w, targets,
    )
    started = call(
        start_kernel, [((2, levels, own + 2 * SUB, LANES), F32)], [VM] * 4,
        crm_state, low, high, courant,
    )
    crm_new, diff = call(
        main_kernel,
        [((2, levels, own, LANES), BF16), ((2, ring * 4, LANES), F32)],
        [VM] * 8,
        arrived, take, take_rank, started, crm_state, courant, cloud_mask, level_down,
        scratch=[
            pltpu.VMEM((2, ring * 4, LANES), F32),
            pltpu.VMEM((levels, LANES), F32),
            pltpu.VMEM((2, levels, own + 2 * SUB, LANES), F32),
        ],
    )
    parts = lax.all_to_all(
        diff.reshape(ring, 8, LANES), "narrow", split_axis=0, concat_axis=0, tiled=True
    )
    back = call(turn_kernel, [((peers, LANES), F32)], [VM] * 2, parts, slots)
    back = lax.all_to_all(
        back.reshape(peers, 1, LANES), "wide", split_axis=0, concat_axis=0, tiled=True
    ).reshape(peers, LANES)
    change = call(back_kernel, [((ring, 8, LANES), F32)], [VM] * 3, back, owner, send_rank)
    change = lax.all_to_all(change, "narrow", split_axis=0, concat_axis=0, tiled=True)
    tendency = call(
        end_kernel, [((width, LANES), BF16)], [VM] * 2,
        change.reshape(ring * 8, LANES), level_up.T,
    )
    return tendency.T, crm_new


def solution(mesh):
    placed = (
        P("wide", None),
        P(None, None, "narrow", "wide"),
        P(None, "wide"),
        P(None, "wide"),
        P(),
        P(),
        P(),
    )
    return jax.shard_map(
        shards,
        mesh=mesh,
        in_specs=placed,
        out_specs=(P("wide", None), P(None, None, "narrow", "wide")),
        check_vma=False,
    )
```

time: 160 us -> 111 us (0.69)
  starting transfers between devices: 79.8 us -> 31.5 us
  Pallas kernels: 0 us -> 18.3 us
  other arithmetic: 11.1 us -> 0 us
  blocking collectives: 42.8 us -> 53.6 us
  waiting for transfers between devices: 13.9 us -> 3.36 us
  local copies, waits for them, and re-layouts: 9.89 us -> 2.45 us
    all_to_all x0 -> x3, blocking collectives: none -> 53.6 us  [the longest x1 21.9 us: shards(): lax.all_to_all(back.reshape(peers, 1, LANES), 'wide', split_axis=0, conca...]
    psum x1 -> x0, blocking collectives: 42.8 us -> none  [shards(): totals = lax.psum(partial_term, 'narrow').astype(jnp.bfloat16)]
    all_to_all x2 -> x1, starting transfers between devices: 44.9 us -> 18.1 us  [shards(): lax.all_to_all(wire.reshape(n // 2, 2, LANES), 'wide', split_axis=0, conc...]
    ppermute x8 -> x2, starting transfers between devices: 34.9 us -> 13.3 us  [the longest x1 11.4 us: shards(): high = lax.ppermute(crm_state[:, :, :SUB], 'narrow', backward)]
    pallas_call x0 -> x7, Pallas kernels: none -> 18.3 us  [call(): pl.pallas_call(kernel, out_shape=out if many else out[0], in_specs=specs,...]
    all_to_all x2 -> x1, waiting for transfers between devices: 10.2 us -> 0.01 us  [shards(): lax.all_to_all(wire.reshape(n // 2, 2, LANES), 'wide', split_axis=0, conc...]
    add x9 -> x0, other arithmetic: 4.99 us -> none  [the longest x4 2.87 us: column_physics(): fields = fields + 0.25 * forcing[:, :, None, :]]
    gather x6 -> x0, local copies, waits for them, and re-layouts: 4.15 us -> none  [the longest x2 1.2 us: shards(): outgoing[send_source]]
  transfers between devices with their start and end apart: 10 -> 3, of which waited for: 4 -> 1; matrix products, arithmetic and copies ran while one was open for 2% -> 1% of each run, Pallas kernels for 0% -> 5%
where the time goes in v1:
time: 111 us; the launch traced here: 110 us
  blocking collectives  53.6 us (48%)
  starting transfers between devices  31.5 us (28%)
  Pallas kernels  18.3 us (16%)
  waiting for transfers between devices  3.36 us (3%)
  local copies, waits for them, and re-layouts  2.45 us (2%)
    all_to_all x1, blocking collectives, shards(): lax.all_to_all(back.reshape(peers, 1, LANES), 'wide', split_axis=0, conca...  21.9 us
    pallas_call x7, Pallas kernels, call(): pl.pallas_call(kernel, out_shape=out if many else out[0], in_specs=specs,...  18.3 us
    all_to_all x1, starting transfers between devices, shards(): lax.all_to_all(wire.reshape(n // 2, 2, LANES), 'wide', split_axis=0, conc...  18.1 us
    all_to_all x1, blocking collectives, shards(): lax.all_to_all(diff.reshape(ring, 8, LANES), 'narrow', split_axis=0, conc...  15.9 us
    all_to_all x1, blocking collectives, shards(): lax.all_to_all(change, 'narrow', split_axis=0, concat_axis=0, tiled=True)  15.8 us
    ppermute x1, starting transfers between devices, shards(): high = lax.ppermute(crm_state[:, :, :SUB], 'narrow', backward)  11.4 us
    ppermute x1, waiting for transfers between devices, shards(): low = lax.ppermute(crm_state[:, :, own - SUB:], 'narrow', forward)  3.35 us
  transfers between devices with their start and end apart: 3, of which 1 were waited for; matrix products, arithmetic and copies ran while one was open for 1% of the time, Pallas kernels for 5%

profile of v1, /device:TPU:1, one launch (start us, length us, event | category | flops | bytes accessed | tf_op | source)
XLA Modules:
  0.0 109.9 jit_solution(5739524443854307471)
XLA Ops:
  0.6 1.9 %shard_map.86 = (bf16[384,128]{1,0:T(8,128)(2,1)}, bf16[64,128]{1,0:T(8,128)(2,1)}, s32[8,128]{1,0:T(8,128)}) custom-call(s32[1]{0:T(128)} %bitcast.w_ref, s32[64,128]{1,0:T(8,128)} %bitcast.16, f32[144,128]{1,0:T(8,128)} %bitcast.20), custom_call_target="tpu_custom_call" | custom-call | tf_op jit(solution)/shard_map/pallas_call | solution.py:251
  2.5 18.1 %all-to-all-start = ((bf16[192,2,128]{2,1,0:T(2,128)(2,1)}), bf16[192,2,128]{2,1,0:T(2,128)(2,1)S(1)}, u32[]{:S(2)}, u32[]{:S(2)}) async-start(bf16[192,2,128]{2,1,0:T(2,128)(2,1)} %bitcast.19), calls=%async_computation | async-start | bytes 196608 | tf_op jit(solution)/shard_map/all_to_all | solution.py:275
  20.7 1.2 %fusion = (bf16[2,60,4,128]{3,2,1,0:T(4,128)(2,1)S(1)}, bf16[2,60,4,128]{3,2,1,0:T(4,128)(2,1)S(1)}) fusion(bf16[2,60,16,128]{3,2,1,0:T(8,128)(2,1)} %crm_ref.3), kind=kLoop, calls=%fused_computation | loop fusion | bytes 491520 | tf_op jit(solution)/shard_map/slice | solution.py:282
  21.9 11.4 %collective-permute-start.1 = (bf16[2,60,4,128]{3,2,1,0:T(4,128)(2,1)S(1)}, bf16[2,60,4,128]{3,2,1,0:T(4,128)(2,1)S(1)}, u32[]{:S(2)}, u32[]{:S(2)}) collective-permute-start(bf16[2,60,4,128]{3,2,1,0:T(4,128)(2,1)S(1)} %get-tuple-element.18), channel_id=1, source_target_pairs={{1,0},{2,1},{3,2},{4,3},{5,4},{6,5},{7,6},{8,7},{9,8},{10,9},{11,1... | collective-permute-start | bytes 368648 | tf_op jit(solution)/shard_map/ppermute | solution.py:282
  33.3 1.9 %collective-permute-start = (bf16[2,60,4,128]{3,2,1,0:T(4,128)(2,1)S(1)}, bf16[2,60,4,128]{3,2,1,0:T(4,128)(2,1)S(1)}, u32[]{:S(2)}, u32[]{:S(2)}) collective-permute-start(bf16[2,60,4,128]{3,2,1,0:T(4,128)(2,1)S(1)} %get-tuple-element.19), channel_id=1, source_target_pairs={{0,1},{1,2},{2,3},{3,4},{4,5},{5,6},{6,7},{7,8},{8,9},{9,10},{10,1... | collective-permute-start | bytes 368648 | tf_op jit(solution)/shard_map/ppermute | solution.py:281
  35.2 2.0 %shard_map.87 = (bf16[64,512]{1,0:T(8,128)(2,1)}, bf16[384,256]{1,0:T(8,128)(2,1)}, s32[8,128]{1,0:T(8,128)}) custom-call(s32[1]{0:T(128)} %bitcast.w_ref, s32[64,128]{1,0:T(8,128)} %bitcast.17), custom_call_target="tpu_custom_call" | custom-call | tf_op jit(solution)/shard_map/pallas_call | solution.py:251
  37.2 0.0 collective-permute-done.1.high_ref
  37.2 0.0 copy-start.1
  37.2 3.4 %collective-permute-done.low_ref = bf16[2,60,4,128]{3,2,1,0:T(4,128)(2,1)S(1)} collective-permute-done((bf16[2,60,4,128]{3,2,1,0:T(4,128)(2,1)S(1)}, bf16[2,60,4,128]{3,2,1,0:T(4,128)(2,1)S(1)}, u32[]{:S(2)}, u32[]{:S(2)}) %collective-permute-start) | collective-permute-done | bytes 122912 | tf_op jit(solution)/shard_map/ppermute | solution.py:281
  40.5 0.0 copy-done.1
  40.5 0.0 copy-start.2
  40.5 0.6 copy-done.2
  41.2 3.1 %shard_map.88.start_ref = f32[2,60,24,128]{3,2,1,0:T(8,128)} custom-call(bf16[2,60,16,128]{3,2,1,0:T(8,128)(2,1)} %crm_ref.3, bf16[2,60,4,128]{3,2,1,0:T(4,128)(2,1)} %copy-done.2, bf16[2,60,4,128]{3,2,1,0:T(4,128)(2,1)} %copy-done.1, f32[60,128]{1,0:T(8,128)} %courant_ref.3), custom_call_target="tpu_custom_call" | custom-call | tf_op jit(solution)/shard_map/pallas_call | solution.py:251
  44.3 0.0 all-to-all-done
  44.3 0.0 copy-start
  44.3 0.6 copy-done
  44.9 6.2 %shard_map.89 = (bf16[2,60,16,128]{3,2,1,0:T(8,128)(2,1)}, f32[2,64,128]{2,1,0:T(8,128)}) custom-call(bf16[384,128]{1,0:T(8,128)(2,1)} %bitcast.13, bf16[384,256]{1,0:T(8,128)(2,1)} %get-tuple-element.11.take_ref, s32[8,128]{1,0:T(8,128)} %get-tuple-element.12.rank_ref, f32[2,60,24,128]{3,2,1,0:T(8,128)} %shard_map.88.start_ref, ...), custom_call_target="tpu_custom_call" | custom-call | tf_op jit(solution)/shard_map/pallas_call | solution.py:251
  51.1 15.9 %all_to_all.20.part_ref = f32[16,8,128]{2,1,0:T(8,128)} all-to-all(f32[16,8,128]{2,1,0:T(8,128)} %bitcast.21), channel_id=1, replica_groups=mesh['wide'=64,'narrow'=16] {'narrow'}, dimensions={0} | all-to-all | bytes 131072 | tf_op jit(solution)/shard_map/all_to_all | solution.py:304
  67.0 1.7 %shard_map.90 = f32[64,128]{1,0:T(8,128)} custom-call(f32[16,8,128]{2,1,0:T(8,128)} %all_to_all.20.part_ref, bf16[64,512]{1,0:T(8,128)(2,1)} %get-tuple-element.14.slot_ref), custom_call_target="tpu_custom_call" | custom-call | tf_op jit(solution)/shard_map/pallas_call | solution.py:251
  68.7 21.9 %all_to_all.21 = f32[64,1,128]{2,1,0:T(1,128)} all-to-all(f32[64,1,128]{2,1,0:T(1,128)} %bitcast.15), channel_id=1, replica_groups=mesh['wide'=64,'narrow'=16] {'wide'}, dimensions={0} | all-to-all | bytes 65536 | tf_op jit(solution)/shard_map/all_to_all | solution.py:308
  90.7 1.6 %shard_map.91 = f32[16,8,128]{2,1,0:T(8,128)} custom-call(f32[64,128]{1,0:T(8,128)} %bitcast.18, bf16[64,128]{1,0:T(8,128)(2,1)} %get-tuple-element.15.owner_ref, s32[8,128]{1,0:T(8,128)} %get-tuple-element.16.rank_ref), custom_call_target="tpu_custom_call" | custom-call | tf_op jit(solution)/shard_map/pallas_call | solution.py:251
  92.3 15.8 %all_to_all.22 = f32[16,8,128]{2,1,0:T(8,128)} all-to-all(f32[16,8,128]{2,1,0:T(8,128)} %shard_map.91), channel_id=1, replica_groups=mesh['wide'=64,'narrow'=16] {'narrow'}, dimensions={0} | all-to-all | bytes 131072 | tf_op jit(solution)/shard_map/all_to_all | solution.py:312
  108.1 1.8 %shard_map.92 = bf16[144,128]{1,0:T(8,128)(2,1)} custom-call(f32[128,128]{1,0:T(8,128)} %bitcast.14, f32[60,72]{1,0:T(8,128)} %bitcast.23), custom_call_target="tpu_custom_call" | custom-call | tf_op jit(solution)/shard_map/pallas_call | solution.py:251
Async XLA Ops:
  2.5 41.8 %all-to-all-start = ((bf16[192,2,128]{2,1,0:T(2,128)(2,1)}), bf16[192,2,128]{2,1,0:T(2,128)(2,1)S(1)}, u32[]{:S(2)}, u32[]{:S(2)}) async-start(bf16[192,2,128]{2,1,0:T(2,128)(2,1)} %bitcast.19), calls=%async_computation | async-start | bytes 196608 | tf_op jit(solution)/shard_map/all_to_all | solution.py:275
  21.9 15.3 %collective-permute-start.1 = (bf16[2,60,4,128]{3,2,1,0:T(4,128)(2,1)S(1)}, bf16[2,60,4,128]{3,2,1,0:T(4,128)(2,1)S(1)}, u32[]{:S(2)}, u32[]{:S(2)}) collective-permute-start(bf16[2,60,4,128]{3,2,1,0:T(4,128)(2,1)S(1)} %get-tuple-element.18), channel_id=1, source_target_pairs={{1,0},{2,1},{3,2},{4,3},{5,4},{6,5},{7,6},{8,7},{9,8},{10,9},{11,1... | collective-permute-start | bytes 368648 | tf_op jit(solution)/shard_map/ppermute | solution.py:282
  33.3 7.2 %collective-permute-start = (bf16[2,60,4,128]{3,2,1,0:T(4,128)(2,1)S(1)}, bf16[2,60,4,128]{3,2,1,0:T(4,128)(2,1)S(1)}, u32[]{:S(2)}, u32[]{:S(2)}) collective-permute-start(bf16[2,60,4,128]{3,2,1,0:T(4,128)(2,1)S(1)} %get-tuple-element.19), channel_id=1, source_target_pairs={{0,1},{1,2},{2,3},{3,4},{4,5},{5,6},{6,7},{7,8},{8,9},{9,10},{10,1... | collective-permute-start | bytes 368648 | tf_op jit(solution)/shard_map/ppermute | solution.py:281
  37.2 3.4 %copy-start.1 = (bf16[2,60,4,128]{3,2,1,0:T(4,128)(2,1)}, bf16[2,60,4,128]{3,2,1,0:T(4,128)(2,1)S(1)}, u32[]{:S(2)}) copy-start(bf16[2,60,4,128]{3,2,1,0:T(4,128)(2,1)S(1)} %collective-permute-done.1.high_ref) | copy-start | bytes 368644
  40.5 0.6 copy-start.2
  44.3 0.6 copy-start

commit v2 on v1

--- a/solution.py
+++ b/solution.py
@@ -1,5 +1,3 @@
-import functools
-
 import jax
 import jax.numpy as jnp
 from jax import lax
@@ -7,12 +5,14 @@
 from jax.experimental.pallas import tpu as pltpu
 from jax.sharding import PartitionSpec as P
 
+
 CX = 256
 SUB = 4
 CAP = 4
 ROWS = 6
 LANES = 128
 EXTRA = 16
+NEAR = 4
 HI = lax.Precision.HIGHEST
 F32 = jnp.float32
 BF16 = jnp.bfloat16
@@ -44,7 +44,20 @@
     return (iota((LANES, LANES), 0) < iota((LANES, LANES), 1)).astype(BF16)
 
 
-def pack_kernel(w_ref, map_ref, state_ref, wire_ref, owner_ref, rank_ref):
+def pack_kernel(
+    w_ref, map_hbm, state_hbm, crm_hbm, courant_hbm, mask_hbm, down_hbm, up_hbm,
+    wire_ref, owner_ref, rank_ref, first_ref, last_ref,
+    map_ref, crm_ref, courant_ref, mask_ref, down_ref, up_ref,
+    state_ref, sems,
+):
+    pairs = (
+        (map_hbm, map_ref), (state_hbm, state_ref), (crm_hbm, crm_ref), (courant_hbm, courant_ref),
+        (mask_hbm, mask_ref), (down_hbm, down_ref), (up_hbm, up_ref),
+    )
+    copies = [pltpu.make_async_copy(a, b, sems.at[i]) for i, (a, b) in enumerate(pairs)]
+    for copy in copies:
+        copy.start()
+    copies[0].wait()
     peers = map_ref.shape[0]
     mine = map_ref[pl.ds(w_ref[0], 1), :] >> 7
     own = iota((peers, LANES), 0) == mine
@@ -58,6 +71,7 @@
     to_peer = peer == mine
     main = (to_peer & (part == rank)).astype(BF16)
     tail = (to_peer & (part == CAP)).astype(BF16)
+    copies[1].wait()
     state = state_ref[...].astype(BF16)
     levels = state.shape[0]
     extra = state[LANES:levels].astype(F32)
@@ -66,6 +80,12 @@
     spread = jnp.concatenate(spread, axis=0).astype(BF16)
     wire = dot(main, state[:LANES], ((1,), (1,))) + dot(tail, spread, ((1,), (1,)))
     wire_ref[...] = wire.astype(BF16)
+    copies[2].wait()
+    own_columns = crm_ref.shape[2]
+    first_ref[...] = crm_ref[:, :, :SUB]
+    last_ref[...] = crm_ref[:, :, own_columns - SUB :]
+    for copy in copies[3:]:
+        copy.wait()
 
 
 def route_kernel(w_ref, map_ref, slot_ref, take_ref, rank_ref):
@@ -212,7 +232,8 @@
             if k:
                 padded.append(jnp.zeros((k * rows, LANES), F32))
             padded.append(piece.astype(F32))
-            padded.append(jnp.zeros((LANES - (k + 1) * rows, LANES), F32))
+            if (k + 1) * rows < LANES:
+                padded.append(jnp.zeros((LANES - (k + 1) * rows, LANES), F32))
             block = jnp.concatenate(padded, axis=0).astype(BF16)
             wire = wire + dot(slot_ref[:, k * LANES : (k + 1) * LANES], block, ((1,), (1,)))
     wire_ref[...] = wire
@@ -230,12 +251,20 @@
     out_ref[...] = jnp.broadcast_to(change[None], out_ref.shape)
 
 
-def end_kernel(change_ref, up_ref, out_ref):
+def end_kernel(part_ref, up_ref, out_ref):
     levels, gcm = up_ref.shape
-    half = change_ref.shape[0] // 2
+    ring, _, _ = part_ref.shape
+    pieces = []
+    for c in range(NEAR):
+        piece = part_ref[c]
+        for g in range(NEAR + c, ring, NEAR):
+            piece = piece + part_ref[g]
+        pieces.append(piece)
+    change = jnp.concatenate(pieces, axis=0)
+    half = change.shape[0] // 2
     for f in range(2):
         tend = lax.dot_general(
-            up_ref[...], change_ref[f * half : f * half + levels], (((0,), (0,)), ((), ())),
+            up_ref[...], change[f * half : f * half + levels], (((0,), (0,)), ((), ())),
             precision=HI, preferred_element_type=F32,
         ) * (1.0 / (CX * SUB))
         out_ref[f * gcm : (f + 1) * gcm] = tend.astype(BF16)
@@ -243,9 +272,10 @@
 
 VM = pl.BlockSpec(memory_space=pltpu.VMEM)
 SM = pl.BlockSpec(memory_space=pltpu.SMEM)
-
-
-def call(kernel, shapes, specs, *args, scratch=()):
+HB = pl.BlockSpec(memory_space=pltpu.HBM)
+
+
+def call(kernel, shapes, specs, *args, scratch=(), room=4):
     out = [jax.ShapeDtypeStruct(s, d) for s, d in shapes]
     many = len(out) > 1
     return pl.pallas_call(
@@ -254,6 +284,7 @@
         in_specs=specs,
         out_specs=[VM] * len(out) if many else VM,
         scratch_shapes=list(scratch),
+        compiler_params=pltpu.CompilerParams(vmem_limit_bytes=room << 20),
     )(*args)
 
 
@@ -266,20 +297,25 @@
     w = lax.axis_index("wide").astype(jnp.int32).reshape(1)
     targets = column_map.reshape(peers, columns)
     n = peers * ROWS
-
-    wire, owner, send_rank = call(
+    near = [[g * NEAR + i for i in range(NEAR)] for g in range(ring // NEAR)]
+    forward = [(i, (i + 1) % ring) for i in range(ring)]
+    backward = [(b, a) for a, b in forward]
+    args = (targets, gcm_state.T, crm_state, courant, cloud_mask, level_down, level_up.T)
+    resident = [(x.shape, x.dtype) for x in args]
+
+    wire, owner, send_rank, first, last, targets, crm, courant, cloud_mask, down, up = call(
         pack_kernel,
-        [((n, LANES), BF16), ((peers, LANES), BF16), ((8, LANES), jnp.int32)],
-        [SM, VM, VM], w, targets, gcm_state.T,
-    )
+        [((n, LANES), BF16), ((peers, LANES), BF16), ((8, LANES), jnp.int32)]
+        + [((2, levels, SUB, LANES), BF16)] * 2
+        + resident[:1] + resident[2:],
+        [SM] + [HB] * 7, w, *[pltpu.with_memory_space_constraint(x, pltpu.HBM) for x in args],
+        scratch=[pltpu.VMEM((width, LANES), F32), pltpu.SemaphoreType.DMA((7,))],
+    )
+    low = lax.ppermute(last, "narrow", forward)
     arrived = lax.all_to_all(
         wire.reshape(n // 2, 2, LANES), "wide", split_axis=0, concat_axis=0, tiled=True
     ).reshape(n, LANES)
-
-    forward = [(i, (i + 1) % ring) for i in range(ring)]
-    backward = [(b, a) for a, b in forward]
-    low = lax.ppermute(crm_state[:, :, own - SUB :], "narrow", forward)
-    high = lax.ppermute(crm_state[:, :, :SUB], "narrow", backward)
+    high = lax.ppermute(first, "narrow", backward)
 
     slots, take, take_rank = call(
         route_kernel,
@@ -288,32 +324,32 @@
     )
     started = call(
         start_kernel, [((2, levels, own + 2 * SUB, LANES), F32)], [VM] * 4,
-        crm_state, low, high, courant,
+        crm, low, high, courant,
     )
     crm_new, diff = call(
         main_kernel,
         [((2, levels, own, LANES), BF16), ((2, ring * 4, LANES), F32)],
         [VM] * 8,
-        arrived, take, take_rank, started, crm_state, courant, cloud_mask, level_down,
+        arrived, take, take_rank, started, crm, courant, cloud_mask, down,
         scratch=[
             pltpu.VMEM((2, ring * 4, LANES), F32),
             pltpu.VMEM((levels, LANES), F32),
             pltpu.VMEM((2, levels, own + 2 * SUB, LANES), F32),
         ],
-    )
+        room=8,
+    )
+    rows = 2 * ring * 4 // NEAR
     parts = lax.all_to_all(
-        diff.reshape(ring, 8, LANES), "narrow", split_axis=0, concat_axis=0, tiled=True
+        diff.reshape(NEAR, rows, LANES), "narrow", split_axis=0, concat_axis=0,
+        axis_index_groups=near, tiled=True,
     )
     back = call(turn_kernel, [((peers, LANES), F32)], [VM] * 2, parts, slots)
     back = lax.all_to_all(
         back.reshape(peers, 1, LANES), "wide", split_axis=0, concat_axis=0, tiled=True
     ).reshape(peers, LANES)
-    change = call(back_kernel, [((ring, 8, LANES), F32)], [VM] * 3, back, owner, send_rank)
+    change = call(back_kernel, [((ring, rows, LANES), F32)], [VM] * 3, back, owner, send_rank)
     change = lax.all_to_all(change, "narrow", split_axis=0, concat_axis=0, tiled=True)
-    tendency = call(
-        end_kernel, [((width, LANES), BF16)], [VM] * 2,
-        change.reshape(ring * 8, LANES), level_up.T,
-    )
+    tendency = call(end_kernel, [((width, LANES), BF16)], [VM] * 2, change, up)
     return tendency.T, crm_new
 
 
@@ -327,6 +363,7 @@
         P(),
         P(),
     )
+
     return jax.shard_map(
         shards,
         mesh=mesh,

time: 111 us -> 97.9 us (0.88)
  the two profiles are of different devices: /device:TPU:1 before, /device:TPU:64 now
where the time goes in v2:
time: 97.9 us; the launch traced here: 97.5 us
  blocking collectives  64.7 us (66%)
  starting transfers between devices  20.7 us (21%)
  Pallas kernels  9.31 us (10%)
  waiting for transfers between devices  2.14 us (2%)
    all_to_all x1, blocking collectives, shards(): lax.all_to_all(change, 'narrow', split_axis=0, concat_axis=0, tiled=True)  28.1 us
    all_to_all x1, blocking collectives, shards(): lax.all_to_all(back.reshape(peers, 1, LANES), 'wide', split_axis=0, conca...  19.8 us
    all_to_all x1, blocking collectives, shards(): lax.all_to_all(diff.reshape(NEAR, rows, LANES), 'narrow', split_axis=0, c...  16.7 us
    all_to_all x1, starting transfers between devices, shards(): lax.all_to_all(wire.reshape(n // 2, 2, LANES), 'wide', split_axis=0, conc...  10.6 us
    pallas_call x7, Pallas kernels, call(): pl.pallas_call(kernel, out_shape=out if many else out[0], in_specs=specs,...  9.31 us
    ppermute x1, starting transfers between devices, shards(): high = lax.ppermute(first, 'narrow', backward)  5.87 us
    ppermute x1, starting transfers between devices, shards(): low = lax.ppermute(last, 'narrow', forward)  4.29 us
  transfers between devices with their start and end apart: 3, of which 2 were waited for; matrix products, arithmetic and copies ran while one was open for 0% of the time, Pallas kernels for 1%

profile of v2, /device:TPU:64, one launch (start us, length us, event | category | flops | bytes accessed | tf_op | source)
XLA Modules:
  0.0 97.5 jit_solution(13372845729168123982)
XLA Ops:
  0.6 2.0 %shard_map.86 = (bf16[384,128]{1,0:T(8,128)(2,1)}, bf16[64,128]{1,0:T(8,128)(2,1)S(1)}, s32[8,128]{1,0:T(8,128)S(1)}, bf16[2,60,4,128]{3,2,1,0:T(4,128)(2,1)S(1)...) custom-call(s32[1]{0:T(128)} %bitcast.w_ref, ...), custom_call_target="tpu_custom_call" | custom-call | tf_op jit(solution)/shard_map/pallas_call | solution.py:281
  2.6 10.6 %all-to-all-start = ((bf16[192,2,128]{2,1,0:T(2,128)(2,1)}), bf16[192,2,128]{2,1,0:T(2,128)(2,1)S(1)}, u32[]{:S(2)}, u32[]{:S(2)}) async-start(bf16[192,2,128]{2,1,0:T(2,128)(2,1)} %bitcast.4), calls=%async_computation | async-start | bytes 196608 | tf_op jit(solution)/shard_map/all_to_all | solution.py:315
  13.2 4.3 %collective-permute-start = (bf16[2,60,4,128]{3,2,1,0:T(4,128)(2,1)S(1)}, bf16[2,60,4,128]{3,2,1,0:T(4,128)(2,1)S(1)}, u32[]{:S(2)}, u32[]{:S(2)}) collective-permute-start(bf16[2,60,4,128]{3,2,1,0:T(4,128)(2,1)S(1)} %get-tuple-element.23), channel_id=1, source_target_pairs={{0,1},{1,2},{2,3},{3,4},{4,5},{5,6},{6,7},{7,8},{8,9},{9,10},{10,1... | collective-permute-start | bytes 368648 | tf_op jit(solution)/shard_map/ppermute | solution.py:314
  17.5 5.9 %collective-permute-start.1 = (bf16[2,60,4,128]{3,2,1,0:T(4,128)(2,1)S(1)}, bf16[2,60,4,128]{3,2,1,0:T(4,128)(2,1)S(1)}, u32[]{:S(2)}, u32[]{:S(2)}) collective-permute-start(bf16[2,60,4,128]{3,2,1,0:T(4,128)(2,1)S(1)} %get-tuple-element.24), channel_id=1, source_target_pairs={{1,0},{2,1},{3,2},{4,3},{5,4},{6,5},{7,6},{8,7},{9,8},{10,9},{11,1... | collective-permute-start | bytes 368648 | tf_op jit(solution)/shard_map/ppermute | solution.py:318
  23.4 0.5 shard_map.87
  23.9 1.0 collective-permute-done.low_ref
  24.8 1.2 %collective-permute-done.1.high_ref = bf16[2,60,4,128]{3,2,1,0:T(4,128)(2,1)S(1)} collective-permute-done((bf16[2,60,4,128]{3,2,1,0:T(4,128)(2,1)S(1)}, bf16[2,60,4,128]{3,2,1,0:T(4,128)(2,1)S(1)}, u32[]{:S(2)}, u32[]{:S(2)}) %collective-permute-start.1) | collective-permute-done | bytes 122912 | tf_op jit(solution)/shard_map/ppermute | solution.py:318
  26.0 0.9 shard_map.88.start_ref
  26.9 0.0 all-to-all-done
  26.9 4.5 %shard_map.89 = (bf16[2,60,16,128]{3,2,1,0:T(8,128)(2,1)}, f32[2,64,128]{2,1,0:T(8,128)S(1)}) custom-call(bf16[384,128]{1,0:T(8,128)(2,1)S(1)} %bitcast.12, bf16[384,256]{1,0:T(8,128)(2,1)S(1)} %get-tuple-element.20.take_ref, s32[8,128]{1,0:T(8,128)S(1)} %get-tuple-element.21.rank_ref, f32[2,60,24,128]{3,2,1,0:T(8,128)S(1)} %shard_map.88.start_ref, ...), custom_call_target="tpu_custom_call" | custom-call | tf_op jit(solution)/shard_map/pallas_call | solution.py:281
  31.5 16.7 %all_to_all.20.part_ref = f32[4,32,128]{2,1,0:T(8,128)S(1)} all-to-all(f32[4,32,128]{2,1,0:T(8,128)S(1)} %bitcast.15), channel_id=1, replica_groups={{0,1,2,3},{4,5,6,7},{8,9,10,11},{12,13,14,15},{16,17,18,19},{20,21,22,2..., dimensions={0} | all-to-all | bytes 131072 | tf_op jit(solution)/shard_map/all_to_all | solution.py:342
  48.2 0.2 shard_map.90
  48.5 19.8 %all_to_all.21 = f32[64,1,128]{2,1,0:T(1,128)S(1)} all-to-all(f32[64,1,128]{2,1,0:T(1,128)S(1)} %bitcast.14), channel_id=1, replica_groups=mesh['wide'=64,'narrow'=16] {'wide'}, dimensions={0} | all-to-all | bytes 65536 | tf_op jit(solution)/shard_map/all_to_all | solution.py:347
  68.3 0.2 shard_map.91
  68.5 28.1 %all_to_all.22.part_ref = f32[16,32,128]{2,1,0:T(8,128)S(1)} all-to-all(f32[16,32,128]{2,1,0:T(8,128)S(1)} %shard_map.91), channel_id=1, replica_groups=mesh['wide'=64,'narrow'=16] {'narrow'}, dimensions={0} | all-to-all | bytes 524288 | tf_op jit(solution)/shard_map/all_to_all | solution.py:351
  96.6 0.9 shard_map.92
Async XLA Ops:
  2.6 24.3 %all-to-all-start = ((bf16[192,2,128]{2,1,0:T(2,128)(2,1)}), bf16[192,2,128]{2,1,0:T(2,128)(2,1)S(1)}, u32[]{:S(2)}, u32[]{:S(2)}) async-start(bf16[192,2,128]{2,1,0:T(2,128)(2,1)} %bitcast.4), calls=%async_computation | async-start | bytes 196608 | tf_op jit(solution)/shard_map/all_to_all | solution.py:315
  13.2 11.7 %collective-permute-start = (bf16[2,60,4,128]{3,2,1,0:T(4,128)(2,1)S(1)}, bf16[2,60,4,128]{3,2,1,0:T(4,128)(2,1)S(1)}, u32[]{:S(2)}, u32[]{:S(2)}) collective-permute-start(bf16[2,60,4,128]{3,2,1,0:T(4,128)(2,1)S(1)} %get-tuple-element.23), channel_id=1, source_target_pairs={{0,1},{1,2},{2,3},{3,4},{4,5},{5,6},{6,7},{7,8},{8,9},{9,10},{10,1... | collective-permute-start | bytes 368648 | tf_op jit(solution)/shard_map/ppermute | solution.py:314
  17.5 8.5 %collective-permute-start.1 = (bf16[2,60,4,128]{3,2,1,0:T(4,128)(2,1)S(1)}, bf16[2,60,4,128]{3,2,1,0:T(4,128)(2,1)S(1)}, u32[]{:S(2)}, u32[]{:S(2)}) collective-permute-start(bf16[2,60,4,128]{3,2,1,0:T(4,128)(2,1)S(1)} %get-tuple-element.24), channel_id=1, source_target_pairs={{1,0},{2,1},{3,2},{4,3},{5,4},{6,5},{7,6},{8,7},{9,8},{10,9},{11,1... | collective-permute-start | bytes 368648 | tf_op jit(solution)/shard_map/ppermute | solution.py:318

commit v3 on v2

--- a/solution.py
+++ b/solution.py
@@ -251,20 +251,16 @@
     out_ref[...] = jnp.broadcast_to(change[None], out_ref.shape)
 
 
-def end_kernel(part_ref, up_ref, out_ref):
+def sum_kernel(part_ref, out_ref):
+    out_ref[...] = jnp.broadcast_to(jnp.sum(part_ref[...], axis=0)[None], out_ref.shape)
+
+
+def end_kernel(change_ref, up_ref, out_ref):
     levels, gcm = up_ref.shape
-    ring, _, _ = part_ref.shape
-    pieces = []
-    for c in range(NEAR):
-        piece = part_ref[c]
-        for g in range(NEAR + c, ring, NEAR):
-            piece = piece + part_ref[g]
-        pieces.append(piece)
-    change = jnp.concatenate(pieces, axis=0)
-    half = change.shape[0] // 2
+    half = change_ref.shape[0] // 2
     for f in range(2):
         tend = lax.dot_general(
-            up_ref[...], change[f * half : f * half + levels], (((0,), (0,)), ((), ())),
+            up_ref[...], change_ref[f * half : f * half + levels], (((0,), (0,)), ((), ())),
             precision=HI, preferred_element_type=F32,
         ) * (1.0 / (CX * SUB))
         out_ref[f * gcm : (f + 1) * gcm] = tend.astype(BF16)
@@ -298,6 +294,7 @@
     targets = column_map.reshape(peers, columns)
     n = peers * ROWS
     near = [[g * NEAR + i for i in range(NEAR)] for g in range(ring // NEAR)]
+    far = [[g + NEAR * i for i in range(ring // NEAR)] for g in range(NEAR)]
     forward = [(i, (i + 1) % ring) for i in range(ring)]
     backward = [(b, a) for a, b in forward]
     args = (targets, gcm_state.T, crm_state, courant, cloud_mask, level_down, level_up.T)
@@ -311,11 +308,11 @@
         [SM] + [HB] * 7, w, *[pltpu.with_memory_space_constraint(x, pltpu.HBM) for x in args],
         scratch=[pltpu.VMEM((width, LANES), F32), pltpu.SemaphoreType.DMA((7,))],
     )
-    low = lax.ppermute(last, "narrow", forward)
+    high = lax.ppermute(first, "narrow", backward)
     arrived = lax.all_to_all(
         wire.reshape(n // 2, 2, LANES), "wide", split_axis=0, concat_axis=0, tiled=True
     ).reshape(n, LANES)
-    high = lax.ppermute(first, "narrow", backward)
+    low = lax.ppermute(last, "narrow", forward)
 
     slots, take, take_rank = call(
         route_kernel,
@@ -347,9 +344,17 @@
     back = lax.all_to_all(
         back.reshape(peers, 1, LANES), "wide", split_axis=0, concat_axis=0, tiled=True
     ).reshape(peers, LANES)
-    change = call(back_kernel, [((ring, rows, LANES), F32)], [VM] * 3, back, owner, send_rank)
-    change = lax.all_to_all(change, "narrow", split_axis=0, concat_axis=0, tiled=True)
-    tendency = call(end_kernel, [((width, LANES), BF16)], [VM] * 2, change, up)
+    change = call(back_kernel, [((NEAR, rows, LANES), F32)], [VM] * 3, back, owner, send_rank)
+    change = lax.all_to_all(
+        change, "narrow", split_axis=0, concat_axis=0, axis_index_groups=far, tiled=True
+    )
+    change = call(sum_kernel, [((NEAR, rows, LANES), F32)], [VM], change)
+    change = lax.all_to_all(
+        change, "narrow", split_axis=0, concat_axis=0, axis_index_groups=near, tiled=True
+    )
+    tendency = call(
+        end_kernel, [((width, LANES), BF16)], [VM] * 2, change.reshape(NEAR * rows, LANES), up
+    )
     return tendency.T, crm_new
 
 

time: 97.9 us -> 101 us (1.032)
  the two profiles are of different devices: /device:TPU:64 before, /device:TPU:1 now
where the time goes in v3:
time: 101 us; the launch traced here: 99.3 us
  blocking collectives  56.1 us (56%)
  starting transfers between devices  31.5 us (31%)
  Pallas kernels  9.31 us (9%)
  waiting for transfers between devices  1.68 us (2%)
    all_to_all x2, blocking collectives, shards(): lax.all_to_all(change, 'narrow', split_axis=0, concat_axis=0, axis_index_...  27.6 us
    all_to_all x1, blocking collectives, shards(): lax.all_to_all(back.reshape(peers, 1, LANES), 'wide', split_axis=0, conca...  21.5 us
    all_to_all x1, starting transfers between devices, shards(): lax.all_to_all(wire.reshape(n // 2, 2, LANES), 'wide', split_axis=0, conc...  18.2 us
    ppermute x1, starting transfers between devices, shards(): high = lax.ppermute(first, 'narrow', backward)  11.4 us
    pallas_call x8, Pallas kernels, call(): pl.pallas_call(kernel, out_shape=out if many else out[0], in_specs=specs,...  9.31 us
    all_to_all x1, blocking collectives, shards(): lax.all_to_all(diff.reshape(NEAR, rows, LANES), 'narrow', split_axis=0, c...  7.05 us
  transfers between devices with their start and end apart: 3, of which 2 were waited for; matrix products, arithmetic and copies ran while one was open for 0% of the time, Pallas kernels for 1%

profile of v3, /device:TPU:1, one launch (start us, length us, event | category | flops | bytes accessed | tf_op | source)
XLA Modules:
  0.0 99.3 jit_solution(15919406803609349902)
XLA Ops:
  0.6 2.0 %shard_map.86 = (bf16[384,128]{1,0:T(8,128)(2,1)}, bf16[64,128]{1,0:T(8,128)(2,1)S(1)}, s32[8,128]{1,0:T(8,128)S(1)}, bf16[2,60,4,128]{3,2,1,0:T(4,128)(2,1)S(1)...) custom-call(s32[1]{0:T(128)} %bitcast.w_ref, ...), custom_call_target="tpu_custom_call" | custom-call | tf_op jit(solution)/shard_map/pallas_call | solution.py:277
  2.6 18.2 %all-to-all-start = ((bf16[192,2,128]{2,1,0:T(2,128)(2,1)}), bf16[192,2,128]{2,1,0:T(2,128)(2,1)S(1)}, u32[]{:S(2)}, u32[]{:S(2)}) async-start(bf16[192,2,128]{2,1,0:T(2,128)(2,1)} %bitcast.4), calls=%async_computation | async-start | bytes 196608 | tf_op jit(solution)/shard_map/all_to_all | solution.py:312
  20.8 1.9 %collective-permute-start = (bf16[2,60,4,128]{3,2,1,0:T(4,128)(2,1)S(1)}, bf16[2,60,4,128]{3,2,1,0:T(4,128)(2,1)S(1)}, u32[]{:S(2)}, u32[]{:S(2)}) collective-permute-start(bf16[2,60,4,128]{3,2,1,0:T(4,128)(2,1)S(1)} %get-tuple-element.23), channel_id=1, source_target_pairs={{0,1},{1,2},{2,3},{3,4},{4,5},{5,6},{6,7},{7,8},{8,9},{9,10},{10,1... | collective-permute-start | bytes 368648 | tf_op jit(solution)/shard_map/ppermute | solution.py:315
  22.7 11.4 %collective-permute-start.1 = (bf16[2,60,4,128]{3,2,1,0:T(4,128)(2,1)S(1)}, bf16[2,60,4,128]{3,2,1,0:T(4,128)(2,1)S(1)}, u32[]{:S(2)}, u32[]{:S(2)}) collective-permute-start(bf16[2,60,4,128]{3,2,1,0:T(4,128)(2,1)S(1)} %get-tuple-element.24), channel_id=1, source_target_pairs={{1,0},{2,1},{3,2},{4,3},{5,4},{6,5},{7,6},{8,7},{9,8},{10,9},{11,1... | collective-permute-start | bytes 368648 | tf_op jit(solution)/shard_map/ppermute | solution.py:311
  34.1 0.5 shard_map.87
  34.6 0.8 collective-permute-done.low_ref
  35.4 0.9 collective-permute-done.1.high_ref
  36.3 0.9 shard_map.88.start_ref
  37.2 0.0 all-to-all-done
  37.2 4.5 %shard_map.89 = (bf16[2,60,16,128]{3,2,1,0:T(8,128)(2,1)}, f32[2,64,128]{2,1,0:T(8,128)S(1)}) custom-call(bf16[384,128]{1,0:T(8,128)(2,1)S(1)} %bitcast.13, bf16[384,256]{1,0:T(8,128)(2,1)S(1)} %get-tuple-element.20.take_ref, s32[8,128]{1,0:T(8,128)S(1)} %get-tuple-element.21.rank_ref, f32[2,60,24,128]{3,2,1,0:T(8,128)S(1)} %shard_map.88.start_ref, ...), custom_call_target="tpu_custom_call" | custom-call | tf_op jit(solution)/shard_map/pallas_call | solution.py:277
  41.8 7.1 %all_to_all.25.part_ref = f32[4,32,128]{2,1,0:T(8,128)S(1)} all-to-all(f32[4,32,128]{2,1,0:T(8,128)S(1)} %bitcast.17), channel_id=1, replica_groups={{0,1,2,3},{4,5,6,7},{8,9,10,11},{12,13,14,15},{16,17,18,19},{20,21,22,2..., dimensions={0} | all-to-all | bytes 131072 | tf_op jit(solution)/shard_map/all_to_all | solution.py:339
  48.8 0.2 shard_map.90
  49.0 21.5 %all_to_all.26 = f32[64,1,128]{2,1,0:T(1,128)S(1)} all-to-all(f32[64,1,128]{2,1,0:T(1,128)S(1)} %bitcast.15), channel_id=1, replica_groups=mesh['wide'=64,'narrow'=16] {'wide'}, dimensions={0} | all-to-all | bytes 65536 | tf_op jit(solution)/shard_map/all_to_all | solution.py:344
  70.5 0.2 shard_map.91
  70.7 20.7 %all_to_all.27.part_ref = f32[4,32,128]{2,1,0:T(8,128)S(1)} all-to-all(f32[4,32,128]{2,1,0:T(8,128)S(1)} %shard_map.91), channel_id=1, replica_groups={{0,4,8,12},{1,5,9,13},{2,6,10,14},{3,7,11,15},{16,20,24,28},{17,21,25,2..., dimensions={0} | all-to-all | bytes 131072 | tf_op jit(solution)/shard_map/all_to_all | solution.py:348
  91.4 7.0 %all_to_all.28 = f32[4,32,128]{2,1,0:T(8,128)S(1)} all-to-all(f32[4,32,128]{2,1,0:T(8,128)S(1)} %shard_map.92), channel_id=1, replica_groups={{0,1,2,3},{4,5,6,7},{8,9,10,11},{12,13,14,15},{16,17,18,19},{20,21,22,2..., dimensions={0} | all-to-all | bytes 131072 | tf_op jit(solution)/shard_map/all_to_all | solution.py:352
  98.4 0.9 shard_map.93
  (1 shorter events, 0.0 us)
Async XLA Ops:
  2.6 34.6 %all-to-all-start = ((bf16[192,2,128]{2,1,0:T(2,128)(2,1)}), bf16[192,2,128]{2,1,0:T(2,128)(2,1)S(1)}, u32[]{:S(2)}, u32[]{:S(2)}) async-start(bf16[192,2,128]{2,1,0:T(2,128)(2,1)} %bitcast.4), calls=%async_computation | async-start | bytes 196608 | tf_op jit(solution)/shard_map/all_to_all | solution.py:312
  20.8 14.6 %collective-permute-start = (bf16[2,60,4,128]{3,2,1,0:T(4,128)(2,1)S(1)}, bf16[2,60,4,128]{3,2,1,0:T(4,128)(2,1)S(1)}, u32[]{:S(2)}, u32[]{:S(2)}) collective-permute-start(bf16[2,60,4,128]{3,2,1,0:T(4,128)(2,1)S(1)} %get-tuple-element.23), channel_id=1, source_target_pairs={{0,1},{1,2},{2,3},{3,4},{4,5},{5,6},{6,7},{7,8},{8,9},{9,10},{10,1... | collective-permute-start | bytes 368648 | tf_op jit(solution)/shard_map/ppermute | solution.py:315
  22.7 13.6 %collective-permute-start.1 = (bf16[2,60,4,128]{3,2,1,0:T(4,128)(2,1)S(1)}, bf16[2,60,4,128]{3,2,1,0:T(4,128)(2,1)S(1)}, u32[]{:S(2)}, u32[]{:S(2)}) collective-permute-start(bf16[2,60,4,128]{3,2,1,0:T(4,128)(2,1)S(1)} %get-tuple-element.24), channel_id=1, source_target_pairs={{1,0},{2,1},{3,2},{4,3},{5,4},{6,5},{7,6},{8,7},{9,8},{10,9},{11,1... | collective-permute-start | bytes 368648 | tf_op jit(solution)/shard_map/ppermute | solution.py:311

commit v4 on v3

--- a/solution.py
+++ b/solution.py
@@ -13,6 +13,11 @@
 LANES = 128
 EXTRA = 16
 NEAR = 4
+SIDE = 0.15
+STEP = 1.0 / (0.1 * SIDE)
+PAD = 8
+PIECES = 3
+UNROLL = 5
 HI = lax.Precision.HIGHEST
 F32 = jnp.float32
 BF16 = jnp.bfloat16
@@ -34,8 +39,8 @@
     return a, b, c
 
 
-def row_parts(n):
-    row = iota((n, LANES), 0)
+def row_parts(start):
+    row = iota((LANES, LANES), 0) + start
     peer = (row * 10923) >> 16
     return peer, row - peer * ROWS
 
@@ -45,8 +50,8 @@
 
 
 def pack_kernel(
-    w_ref, map_hbm, state_hbm, crm_hbm, courant_hbm, mask_hbm, down_hbm, up_hbm,
-    wire_ref, owner_ref, rank_ref, first_ref, last_ref,
+    place_ref, map_hbm, state_hbm, crm_hbm, courant_hbm, mask_hbm, down_hbm, up_hbm,
+    wire_ref, owner_ref, rank_ref, face_ref, other_ref,
     map_ref, crm_ref, courant_ref, mask_ref, down_ref, up_ref,
     state_ref, sems,
 ):
@@ -59,18 +64,13 @@
         copy.start()
     copies[0].wait()
     peers = map_ref.shape[0]
-    mine = map_ref[pl.ds(w_ref[0], 1), :] >> 7
+    mine = map_ref[pl.ds(place_ref[0], 1), :] >> 7
     own = iota((peers, LANES), 0) == mine
     own_b = own.astype(BF16)
     count = dot(own_b, before_matrix(), ((1,), (0,)))
     rank = jnp.sum(jnp.where(own, count, 0.0), axis=0, keepdims=True).astype(jnp.int32)
     owner_ref[...] = own_b
     rank_ref[...] = jnp.broadcast_to(rank, rank_ref.shape)
-    n = peers * ROWS
-    peer, part = row_parts(n)
-    to_peer = peer == mine
-    main = (to_peer & (part == rank)).astype(BF16)
-    tail = (to_peer & (part == CAP)).astype(BF16)
     copies[1].wait()
     state = state_ref[...].astype(BF16)
     levels = state.shape[0]
@@ -78,20 +78,47 @@
     spread = [jnp.where(rank == k, extra, 0.0) for k in range(CAP)]
     spread.append(jnp.zeros((LANES - CAP * EXTRA, LANES), F32))
     spread = jnp.concatenate(spread, axis=0).astype(BF16)
-    wire = dot(main, state[:LANES], ((1,), (1,))) + dot(tail, spread, ((1,), (1,)))
-    wire_ref[...] = wire.astype(BF16)
+    for start in range(0, peers * ROWS, LANES):
+        peer, part = row_parts(start)
+        to_peer = peer == mine
+        main = (to_peer & (part == rank)).astype(BF16)
+        tail = (to_peer & (part == CAP)).astype(BF16)
+        wire = dot(main, state[:LANES], ((1,), (1,))) + dot(tail, spread, ((1,), (1,)))
+        wire_ref[start : start + LANES] = wire.astype(BF16)
     copies[2].wait()
     own_columns = crm_ref.shape[2]
-    first_ref[...] = crm_ref[:, :, :SUB]
-    last_ref[...] = crm_ref[:, :, own_columns - SUB :]
+    odd = (place_ref[1] & 1) == 1
+
+    def faces(to_low, to_high):
+        def body(level, carry):
+            for f in range(2):
+                to_low[f, level] = crm_ref[f, level, :SUB]
+                to_high[f, level] = crm_ref[f, level, own_columns - SUB :]
+            return carry
+
+        lax.fori_loop(0, crm_ref.shape[1], body, 0, unroll=UNROLL)
+
+    @pl.when(odd)
+    def _():
+        faces(face_ref, other_ref)
+
+    @pl.when(jnp.logical_not(odd))
+    def _():
+        faces(other_ref, face_ref)
+
     for copy in copies[3:]:
         copy.wait()
 
 
-def route_kernel(w_ref, map_ref, slot_ref, take_ref, rank_ref):
+def route_kernel(
+    place_ref, map_ref, courant_ref, mask_ref, slot_ref, take_ref, rank_ref, left_ref, here_ref, cloud_ref
+):
+    left_ref[...] = courant_ref[...] * (1.0 / SIDE) + 1.0
+    here_ref[...] = (0.7 - courant_ref[...]) * (1.0 / SIDE)
+    cloud_ref[...] = mask_ref[...].astype(F32) * 0.3
     peers = map_ref.shape[0]
     targets = map_ref[...]
-    here = (targets >> 7) == w_ref[0]
+    here = (targets >> 7) == place_ref[0]
     local = (targets & (LANES - 1)).astype(F32) + 1.0
     count = dot(here.astype(BF16), before_matrix(), ((1,), (0,)))
     slots = []
@@ -120,105 +147,143 @@
     take_ref[:, LANES:] = tail.astype(BF16)
 
 
-def horizontal(x, a0, a1, keep=None):
+def mix(ref, f, level, left, here, rows):
+    return (
+        left * ref[f, level, PAD - 1 : PAD - 1 + rows]
+        + here * ref[f, level, PAD : PAD + rows]
+        + ref[f, level, PAD + 1 : PAD + 1 + rows]
+    )
+
+
+def put(ref, f, level, x):
     n = x.shape[0]
-    left = pltpu.roll(x, 1, 0)
-    right = pltpu.roll(x, n - 1, 0)
-    if keep is not None:
-        left, x, right = left[:keep], x[:keep], right[:keep]
-    return a1 * left + a0 * x + 0.15 * right
-
-
-def start_kernel(crm_ref, low_ref, high_ref, courant_ref, out_ref):
-    levels = crm_ref.shape[1]
-
-    def mixed(level):
-        c = courant_ref[pl.ds(level, 1), :]
-        a0, a1 = 0.7 - c, c + 0.15
-        result = []
-        for f in range(2):
-            x = jnp.concatenate(
-                [
-                    crm_ref[f, level].astype(F32),
-                    high_ref[f, level].astype(F32),
-                    low_ref[f, level].astype(F32),
-                ],
-                axis=0,
-            )
-            result.append(horizontal(x, a0, a1))
-        return tuple(result)
-
+    ref[f, level, PAD : PAD + n] = x
+    ref[f, level, PAD - 1 : PAD] = x[n - 1 :]
+    ref[f, level, PAD + n : PAD + n + 1] = x[:1]
+
+
+def column(levels, mixed, keep):
     def body(level, carry):
         below, here = carry
         above = mixed(jnp.minimum(level + 1, levels - 1))
+        keep(level, [8.0 * h + (a + b) for a, h, b in zip(above, here, below, strict=True)])
+        return here, above
+
+    start = mixed(0)
+    return body, (start, start)
+
+
+def start_kernel(place_ref, crm_ref, near_ref, far_ref, left_ref, here_ref, out_ref, load_ref):
+    levels = crm_ref.shape[1]
+    odd = (place_ref[1] & 1) == 1
+
+    def load(level, carry):
+        fields = []
         for f in range(2):
-            out_ref[f, level] = 0.8 * here[f] + 0.1 * (above[f] + below[f])
-        return here, above
-
-    first = mixed(0)
-    lax.fori_loop(0, levels, body, (first, first), unroll=4)
+            near = near_ref[f, level].astype(F32)
+            far = far_ref[f, level].astype(F32)
+            halo = jnp.where(
+                odd, jnp.concatenate([far, near], axis=0), jnp.concatenate([near, far], axis=0)
+            )
+            fields.append(jnp.concatenate([crm_ref[f, level].astype(F32), halo], axis=0))
+        put(load_ref, 0, level, fields[0] + 2.0 * fields[1])
+        put(load_ref, 1, level, fields[1])
+        return carry
+
+    lax.fori_loop(0, levels, load, 0, unroll=UNROLL)
+    rows = out_ref.shape[2]
+
+    def mixed(level):
+        left, here = left_ref[pl.ds(level, 1), :], here_ref[pl.ds(level, 1), :]
+        return tuple(mix(load_ref, f, level, left, here, rows) for f in range(2))
+
+    def keep(level, pair):
+        for f in range(2):
+            out_ref[f, level] = pair[f]
+
+    body, carry = column(levels, mixed, keep)
+    lax.fori_loop(0, levels, body, carry, unroll=UNROLL)
 
 
 def main_kernel(
-    wire_ref, take_ref, rank_ref, start_ref, crm_ref, courant_ref, mask_ref, down_ref,
-    new_ref, diff_ref, force_ref, cloud_ref, field_ref,
+    wire_ref, take_ref, rank_ref, start_ref, crm_ref, left_ref, here_ref, cloud_ref, down_ref,
+    new_hbm, diff_ref, force_ref, field_ref, next_ref, new_ref, sems,
 ):
     levels = crm_ref.shape[1]
     gcm = down_ref.shape[1]
     own = crm_ref.shape[2]
+    full = start_ref.shape[2]
     got = dot(wire_ref[...], take_ref[...], ((0,), (0,)))
     tail = jnp.zeros((EXTRA, LANES), F32)
     rank = rank_ref[0:1, :]
     for k in range(CAP):
         tail = tail + jnp.where(rank == k, got[k * EXTRA : (k + 1) * EXTRA, LANES:], 0.0)
     rows = jnp.concatenate([got[:, :LANES], tail], axis=0)
-    for f in range(2):
-        force = lax.dot_general(
+    force = [
+        lax.dot_general(
             down_ref[...], rows[f * gcm : (f + 1) * gcm], (((1,), (0,)), ((), ())),
             precision=HI, preferred_element_type=F32,
         )
-        force_ref[f, :levels] = 0.25 * force
-    cloud_ref[...] = mask_ref[...].astype(F32) * 0.3
-    diff_ref[...] = jnp.zeros_like(diff_ref)
-
-    def physics(pair, level):
-        t = pair[0] + force_ref[0, pl.ds(level, 1), :]
-        q = pair[1] + force_ref[1, pl.ds(level, 1), :]
-        condensed = cloud_ref[pl.ds(level, 1), :] * jnp.maximum(q, 0.0)
-        return t + 2.0 * condensed, q - condensed
-
-    def substep(index):
-        source = start_ref if index == 1 else field_ref
+        for f in range(2)
+    ]
+    force[0] = force[0] + 2.0 * force[1]
+    for index in range(SUB):
+        for f in range(2):
+            force_ref[index, f, :levels] = (0.25 * STEP ** (index + 1)) * force[f]
+    diff_ref[:, levels:] = jnp.zeros((2, diff_ref.shape[1] - levels, LANES), F32)
+
+    def physics(pair, level, index):
+        m = pair[0] + force_ref[index, 0, pl.ds(level, 1), :]
+        q = pair[1] + force_ref[index, 1, pl.ds(level, 1), :]
+        return m, q - cloud_ref[pl.ds(level, 1), :] * jnp.maximum(q, 0.0)
+
+    def first(level, carry):
+        pair = physics((start_ref[0, level], start_ref[1, level]), level, 0)
+        for f in range(2):
+            put(field_ref, f, level, pair[f])
+        return carry
+
+    lax.fori_loop(0, levels, first, 0, unroll=UNROLL)
+    piece = levels // PIECES
+    copies = []
+    for index in range(1, SUB):
         last = index == SUB - 1
-        keep = own if last else None
-
-        def mixed(level):
-            c = courant_ref[pl.ds(level, 1), :]
-            a0, a1 = 0.7 - c, c + 0.15
-            pair = (source[0, level], source[1, level])
-            if index == 1:
-                pair = physics(pair, level)
-            return tuple(horizontal(x, a0, a1, keep) for x in pair)
-
-        def body(level, carry):
-            below, here = carry
-            above = mixed(jnp.minimum(level + 1, levels - 1))
-            pair = tuple(0.8 * here[f] + 0.1 * (above[f] + below[f]) for f in range(2))
-            pair = physics(pair, level)
+        source, target = (field_ref, next_ref) if index % 2 else (next_ref, field_ref)
+        size = own if last else full
+
+        def mixed(level, source=source, size=size):
+            left, here = left_ref[pl.ds(level, 1), :], here_ref[pl.ds(level, 1), :]
+            return tuple(mix(source, f, level, left, here, size) for f in range(2))
+
+        def keep(level, pair, index=index, last=last, target=target):
+            pair = physics(pair, level, index)
+            if not last:
+                for f in range(2):
+                    put(target, f, level, pair[f])
+                return
+            scale = STEP**-SUB
+            q = scale * pair[1]
+            t = scale * pair[0] - 2.0 * q
+            for f, x in enumerate((t, q)):
+                new_ref[f, level] = x.astype(BF16)
+                change = x - crm_ref[f, level].astype(F32)
+                diff_ref[f, pl.ds(level, 1), :] = jnp.sum(change, axis=0, keepdims=True)
+
+        body, carry = column(levels, mixed, keep)
+        if not last:
+            lax.fori_loop(0, levels, body, carry, unroll=UNROLL)
+            continue
+        for part in range(PIECES):
+            carry = lax.fori_loop(part * piece, (part + 1) * piece, body, carry, unroll=UNROLL)
+            span = pl.ds(part * piece, piece)
             for f in range(2):
-                if last:
-                    new_ref[f, level] = pair[f].astype(BF16)
-                    change = pair[f] - crm_ref[f, level].astype(F32)
-                    diff_ref[f, pl.ds(level, 1), :] = jnp.sum(change, axis=0, keepdims=True)
-                else:
-                    field_ref[f, level] = pair[f]
-            return here, above
-
-        first = mixed(0)
-        lax.fori_loop(0, levels, body, (first, first), unroll=4)
-
-    for index in range(1, SUB):
-        substep(index)
+                copy = pltpu.make_async_copy(
+                    new_ref.at[f, span], new_hbm.at[f, span], sems.at[2 * part + f]
+                )
+                copy.start()
+                copies.append(copy)
+    for copy in copies:
+        copy.wait()
 
 
 def turn_kernel(part_ref, slot_ref, wire_ref):
@@ -271,14 +336,14 @@
 HB = pl.BlockSpec(memory_space=pltpu.HBM)
 
 
-def call(kernel, shapes, specs, *args, scratch=(), room=4):
+def call(kernel, shapes, specs, *args, scratch=(), room=4, outs=None):
     out = [jax.ShapeDtypeStruct(s, d) for s, d in shapes]
     many = len(out) > 1
     return pl.pallas_call(
         kernel,
         out_shape=out if many else out[0],
         in_specs=specs,
-        out_specs=[VM] * len(out) if many else VM,
+        out_specs=outs or ([VM] * len(out) if many else VM),
         scratch_shapes=list(scratch),
         compiler_params=pltpu.CompilerParams(vmem_limit_bytes=room << 20),
     )(*args)
@@ -290,50 +355,59 @@
     columns, width = gcm_state.shape
     levels = crm_state.shape[1]
     own = crm_state.shape[2]
-    w = lax.axis_index("wide").astype(jnp.int32).reshape(1)
+    place = jnp.stack([lax.axis_index("wide"), lax.axis_index("narrow")]).astype(jnp.int32)
     targets = column_map.reshape(peers, columns)
     n = peers * ROWS
     near = [[g * NEAR + i for i in range(NEAR)] for g in range(ring // NEAR)]
     far = [[g + NEAR * i for i in range(ring // NEAR)] for g in range(NEAR)]
-    forward = [(i, (i + 1) % ring) for i in range(ring)]
-    backward = [(b, a) for a, b in forward]
+    pairs = [(i, i ^ 1) for i in range(ring)]
+    other_pairs = [(i, ((i + 1) ^ 1) - 1) for i in range(ring)]
+    other_pairs = [(a, b % ring) for a, b in other_pairs]
     args = (targets, gcm_state.T, crm_state, courant, cloud_mask, level_down, level_up.T)
     resident = [(x.shape, x.dtype) for x in args]
 
-    wire, owner, send_rank, first, last, targets, crm, courant, cloud_mask, down, up = call(
+    wire, owner, send_rank, face, other, targets, crm, courant, cloud_mask, down, up = call(
         pack_kernel,
         [((n, LANES), BF16), ((peers, LANES), BF16), ((8, LANES), jnp.int32)]
         + [((2, levels, SUB, LANES), BF16)] * 2
         + resident[:1] + resident[2:],
-        [SM] + [HB] * 7, w, *[pltpu.with_memory_space_constraint(x, pltpu.HBM) for x in args],
+        [SM] + [HB] * 7, place, *[pltpu.with_memory_space_constraint(x, pltpu.HBM) for x in args],
         scratch=[pltpu.VMEM((width, LANES), F32), pltpu.SemaphoreType.DMA((7,))],
     )
-    high = lax.ppermute(first, "narrow", backward)
     arrived = lax.all_to_all(
         wire.reshape(n // 2, 2, LANES), "wide", split_axis=0, concat_axis=0, tiled=True
     ).reshape(n, LANES)
-    low = lax.ppermute(last, "narrow", forward)
-
-    slots, take, take_rank = call(
+    halo_near = lax.ppermute(face, "narrow", pairs)
+    halo_far = lax.ppermute(other, "narrow", other_pairs)
+
+    slots, take, take_rank, left, here, cloud = call(
         route_kernel,
-        [((peers, CAP * LANES), BF16), ((n, 2 * LANES), BF16), ((8, LANES), jnp.int32)],
-        [SM, VM], w, targets,
-    )
+        [((peers, CAP * LANES), BF16), ((n, 2 * LANES), BF16), ((8, LANES), jnp.int32)]
+        + [((levels, LANES), F32)] * 3,
+        [SM] + [VM] * 3, place, targets, courant, cloud_mask,
+    )
+    full = own + 2 * SUB
+    padded = full + 2 * PAD
     started = call(
-        start_kernel, [((2, levels, own + 2 * SUB, LANES), F32)], [VM] * 4,
-        crm, low, high, courant,
+        start_kernel, [((2, levels, full, LANES), F32)], [SM] + [VM] * 5,
+        place, crm, halo_near, halo_far, left, here,
+        scratch=[pltpu.VMEM((2, levels, padded, LANES), F32)],
+        room=6,
     )
     crm_new, diff = call(
         main_kernel,
         [((2, levels, own, LANES), BF16), ((2, ring * 4, LANES), F32)],
-        [VM] * 8,
-        arrived, take, take_rank, started, crm, courant, cloud_mask, down,
+        [VM] * 9,
+        arrived, take, take_rank, started, crm, left, here, cloud, down,
         scratch=[
-            pltpu.VMEM((2, ring * 4, LANES), F32),
-            pltpu.VMEM((levels, LANES), F32),
-            pltpu.VMEM((2, levels, own + 2 * SUB, LANES), F32),
+            pltpu.VMEM((SUB, 2, ring * 4, LANES), F32),
+            pltpu.VMEM((2, levels, padded, LANES), F32),
+            pltpu.VMEM((2, levels, padded, LANES), F32),
+            pltpu.VMEM((2, levels, own, LANES), BF16),
+            pltpu.SemaphoreType.DMA((2 * PIECES,)),
         ],
-        room=8,
+        room=12,
+        outs=[HB, VM],
     )
     rows = 2 * ring * 4 // NEAR
     parts = lax.all_to_all(

time: 101 us -> 100 us (0.990)
  blocking collectives: 56.1 us -> 54.2 us
    all_to_all x2, blocking collectives: 27.6 us -> 25.7 us  [shards(): lax.all_to_all(change, 'narrow', split_axis=0, concat_axis=0, axis_index_...]
  transfers between devices with their start and end apart: 3 -> 3, of which waited for: 2 -> 1; matrix products, arithmetic and copies ran while one was open for 0% -> 0% of each run, Pallas kernels for 1% -> 2%
where the time goes in v4:
time: 100 us; the launch traced here: 98.4 us
  blocking collectives  54.2 us (54%)
  starting transfers between devices  31.7 us (32%)
  Pallas kernels  9.76 us (10%)
  waiting for transfers between devices  1.87 us (2%)
    all_to_all x2, blocking collectives, shards(): lax.all_to_all(change, 'narrow', split_axis=0, concat_axis=0, axis_index_...  25.7 us
    all_to_all x1, blocking collectives, shards(): lax.all_to_all(back.reshape(peers, 1, LANES), 'wide', split_axis=0, conca...  21.5 us
    all_to_all x1, starting transfers between devices, shards(): lax.all_to_all(wire.reshape(n // 2, 2, LANES), 'wide', split_axis=0, conc...  18.2 us
    ppermute x1, starting transfers between devices, shards(): halo_far = lax.ppermute(other, 'narrow', other_pairs)  11.6 us
    pallas_call x8, Pallas kernels, call(): pl.pallas_call(kernel, out_shape=out if many else out[0], in_specs=specs,...  9.76 us
    all_to_all x1, blocking collectives, shards(): lax.all_to_all(diff.reshape(NEAR, rows, LANES), 'narrow', split_axis=0, c...  7.06 us
  transfers between devices with their start and end apart: 3, of which 1 were waited for; matrix products, arithmetic and copies ran while one was open for 0% of the time, Pallas kernels for 2%

profile of v4, /device:TPU:1, one launch (start us, length us, event | category | flops | bytes accessed | tf_op | source)
XLA Modules:
  0.0 98.4 jit_solution(10939827979748072029)
XLA Ops:
  0.6 0.1 pad_add_fusion.place_ref
  0.7 2.6 %shard_map.86 = (bf16[384,128]{1,0:T(8,128)(2,1)}, bf16[64,128]{1,0:T(8,128)(2,1)S(1)}, s32[8,128]{1,0:T(8,128)S(1)}, bf16[2,60,4,128]{3,2,1,0:T(4,128)(2,1)S(1)...) custom-call(s32[2]{0:T(128)S(1)} %pad_add_fusion.place_ref, ...), custom_call_target="tpu_custom_call" | custom-call | tf_op jit(solution)/shard_map/pallas_call | solution.py:342
  3.3 18.2 %all-to-all-start = ((bf16[192,2,128]{2,1,0:T(2,128)(2,1)}), bf16[192,2,128]{2,1,0:T(2,128)(2,1)S(1)}, u32[]{:S(2)}, u32[]{:S(2)}) async-start(bf16[192,2,128]{2,1,0:T(2,128)(2,1)} %bitcast.5), calls=%async_computation | async-start | bytes 196608 | tf_op jit(solution)/shard_map/all_to_all | solution.py:377
  21.5 1.9 %collective-permute-start = (bf16[2,60,4,128]{3,2,1,0:T(4,128)(2,1)S(1)}, bf16[2,60,4,128]{3,2,1,0:T(4,128)(2,1)S(1)}, u32[]{:S(2)}, u32[]{:S(2)}) collective-permute-start(bf16[2,60,4,128]{3,2,1,0:T(4,128)(2,1)S(1)} %get-tuple-element.28), channel_id=1, source_target_pairs={{0,1},{1,0},{2,3},{3,2},{4,5},{5,4},{6,7},{7,6},{8,9},{9,8},{10,11... | collective-permute-start | bytes 368648 | tf_op jit(solution)/shard_map/ppermute | solution.py:380
  23.4 11.6 %collective-permute-start.1 = (bf16[2,60,4,128]{3,2,1,0:T(4,128)(2,1)S(1)}, bf16[2,60,4,128]{3,2,1,0:T(4,128)(2,1)S(1)}, u32[]{:S(2)}, u32[]{:S(2)}) collective-permute-start(bf16[2,60,4,128]{3,2,1,0:T(4,128)(2,1)S(1)} %get-tuple-element.29), channel_id=1, source_target_pairs={{0,15},{1,2},{2,1},{3,4},{4,3},{5,6},{6,5},{7,8},{8,7},{9,10},{10,... | collective-permute-start | bytes 368648 | tf_op jit(solution)/shard_map/ppermute | solution.py:381
  35.0 1.1 %shard_map.87 = (bf16[64,512]{1,0:T(8,128)(2,1)S(1)}, bf16[384,256]{1,0:T(8,128)(2,1)S(1)}, s32[8,128]{1,0:T(8,128)S(1)}, f32[60,128]{1,0:T(8,128)S(1)}, f32[60,128]{1,0:T(8,128)S(1)}, /*index=5*/f32[60,128]{1,0:T(8,128)S(1)}) custom-call(s32[2]{0:T(128)S(1)} %pad_add_fusion.place_ref, s32[64,128]{1,0:T(8,128)S(1)} %get-tuple-element.22.map_ref, ...), custom_call_target="tpu_custom_call" | custom-call | tf_op jit(solution)/shard_map/pallas_call | solution.py:342
  36.1 0.0 collective-permute-done.near_ref
  36.1 1.9 %collective-permute-done.1.far_ref = bf16[2,60,4,128]{3,2,1,0:T(4,128)(2,1)S(1)} collective-permute-done((bf16[2,60,4,128]{3,2,1,0:T(4,128)(2,1)S(1)}, bf16[2,60,4,128]{3,2,1,0:T(4,128)(2,1)S(1)}, u32[]{:S(2)}, u32[]{:S(2)}) %collective-permute-start.1) | collective-permute-done | bytes 122912 | tf_op jit(solution)/shard_map/ppermute | solution.py:381
  38.0 1.3 %shard_map.88.start_ref = f32[2,60,24,128]{3,2,1,0:T(8,128)S(1)} custom-call(s32[2]{0:T(128)S(1)} %pad_add_fusion.place_ref, bf16[2,60,16,128]{3,2,1,0:T(8,128)(2,1)S(1)} %get-tuple-element.27.crm_ref, bf16[2,60,4,128]{3,2,1,0:T(4,128)(2,1)S(1)} %collective-permute-done.near_ref, bf16[2,60,4,128]{3,2,1,0:T(4,128)(2,1)S(1)} %collective-permute-done.1.far_ref, ...), custom_call_target="tpu_custom_call" | custom-call | tf_op jit(solution)/shard_map/pallas_call | solution.py:342
  39.3 0.0 all-to-all-done
  39.3 3.4 %shard_map.89 = (bf16[2,60,16,128]{3,2,1,0:T(8,128)(2,1)}, f32[2,64,128]{2,1,0:T(8,128)S(1)}) custom-call(bf16[384,128]{1,0:T(8,128)(2,1)S(1)} %bitcast.14, bf16[384,256]{1,0:T(8,128)(2,1)S(1)} %get-tuple-element.25.take_ref, s32[8,128]{1,0:T(8,128)S(1)} %get-tuple-element.26.rank_ref, f32[2,60,24,128]{3,2,1,0:T(8,128)S(1)} %shard_map.88.start_ref, ...), custom_call_target="tpu_custom_call" | custom-call | tf_op jit(solution)/shard_map/pallas_call | solution.py:342
  42.7 7.1 %all_to_all.25.part_ref = f32[4,32,128]{2,1,0:T(8,128)S(1)} all-to-all(f32[4,32,128]{2,1,0:T(8,128)S(1)} %bitcast.18), channel_id=1, replica_groups={{0,1,2,3},{4,5,6,7},{8,9,10,11},{12,13,14,15},{16,17,18,19},{20,21,22,2..., dimensions={0} | all-to-all | bytes 131072 | tf_op jit(solution)/shard_map/all_to_all | solution.py:413
  49.8 0.2 shard_map.90
  50.0 21.5 %all_to_all.26 = f32[64,1,128]{2,1,0:T(1,128)S(1)} all-to-all(f32[64,1,128]{2,1,0:T(1,128)S(1)} %bitcast.16), channel_id=1, replica_groups=mesh['wide'=64,'narrow'=16] {'wide'}, dimensions={0} | all-to-all | bytes 65536 | tf_op jit(solution)/shard_map/all_to_all | solution.py:418
  71.5 0.2 shard_map.91
  71.8 18.7 %all_to_all.27.part_ref = f32[4,32,128]{2,1,0:T(8,128)S(1)} all-to-all(f32[4,32,128]{2,1,0:T(8,128)S(1)} %shard_map.91), channel_id=1, replica_groups={{0,4,8,12},{1,5,9,13},{2,6,10,14},{3,7,11,15},{16,20,24,28},{17,21,25,2..., dimensions={0} | all-to-all | bytes 131072 | tf_op jit(solution)/shard_map/all_to_all | solution.py:422
  90.5 7.0 %all_to_all.28 = f32[4,32,128]{2,1,0:T(8,128)S(1)} all-to-all(f32[4,32,128]{2,1,0:T(8,128)S(1)} %shard_map.92), channel_id=1, replica_groups={{0,1,2,3},{4,5,6,7},{8,9,10,11},{12,13,14,15},{16,17,18,19},{20,21,22,2..., dimensions={0} | all-to-all | bytes 131072 | tf_op jit(solution)/shard_map/all_to_all | solution.py:426
  97.4 0.9 shard_map.93
  (1 shorter events, 0.0 us)
Async XLA Ops:
  3.3 36.0 %all-to-all-start = ((bf16[192,2,128]{2,1,0:T(2,128)(2,1)}), bf16[192,2,128]{2,1,0:T(2,128)(2,1)S(1)}, u32[]{:S(2)}, u32[]{:S(2)}) async-start(bf16[192,2,128]{2,1,0:T(2,128)(2,1)} %bitcast.5), calls=%async_computation | async-start | bytes 196608 | tf_op jit(solution)/shard_map/all_to_all | solution.py:377
  21.5 14.7 %collective-permute-start = (bf16[2,60,4,128]{3,2,1,0:T(4,128)(2,1)S(1)}, bf16[2,60,4,128]{3,2,1,0:T(4,128)(2,1)S(1)}, u32[]{:S(2)}, u32[]{:S(2)}) collective-permute-start(bf16[2,60,4,128]{3,2,1,0:T(4,128)(2,1)S(1)} %get-tuple-element.28), channel_id=1, source_target_pairs={{0,1},{1,0},{2,3},{3,2},{4,5},{5,4},{6,7},{7,6},{8,9},{9,8},{10,11... | collective-permute-start | bytes 368648 | tf_op jit(solution)/shard_map/ppermute | solution.py:380
  23.4 14.6 %collective-permute-start.1 = (bf16[2,60,4,128]{3,2,1,0:T(4,128)(2,1)S(1)}, bf16[2,60,4,128]{3,2,1,0:T(4,128)(2,1)S(1)}, u32[]{:S(2)}, u32[]{:S(2)}) collective-permute-start(bf16[2,60,4,128]{3,2,1,0:T(4,128)(2,1)S(1)} %get-tuple-element.29), channel_id=1, source_target_pairs={{0,15},{1,2},{2,1},{3,4},{4,3},{5,6},{6,5},{7,8},{8,7},{9,10},{10,... | collective-permute-start | bytes 368648 | tf_op jit(solution)/shard_map/ppermute | solution.py:381

commit v5 on v4

--- a/solution.py
+++ b/solution.py
@@ -50,7 +50,7 @@
 
 
 def pack_kernel(
-    place_ref, map_hbm, state_hbm, crm_hbm, courant_hbm, mask_hbm, down_hbm, up_hbm,
+    map_hbm, state_hbm, crm_hbm, courant_hbm, mask_hbm, down_hbm, up_hbm,
     wire_ref, owner_ref, rank_ref, face_ref, other_ref,
     map_ref, crm_ref, courant_ref, mask_ref, down_ref, up_ref,
     state_ref, sems,
@@ -64,7 +64,7 @@
         copy.start()
     copies[0].wait()
     peers = map_ref.shape[0]
-    mine = map_ref[pl.ds(place_ref[0], 1), :] >> 7
+    mine = map_ref[pl.ds(lax.axis_index("wide"), 1), :] >> 7
     own = iota((peers, LANES), 0) == mine
     own_b = own.astype(BF16)
     count = dot(own_b, before_matrix(), ((1,), (0,)))
@@ -87,7 +87,7 @@
         wire_ref[start : start + LANES] = wire.astype(BF16)
     copies[2].wait()
     own_columns = crm_ref.shape[2]
-    odd = (place_ref[1] & 1) == 1
+    odd = (lax.axis_index("narrow") & 1) == 1
 
     def faces(to_low, to_high):
         def body(level, carry):
@@ -111,14 +111,26 @@
 
 
 def route_kernel(
-    place_ref, map_ref, courant_ref, mask_ref, slot_ref, take_ref, rank_ref, left_ref, here_ref, cloud_ref
+    map_ref, crm_ref, courant_ref, mask_ref,
+    slot_ref, take_ref, rank_ref, left_ref, here_ref, cloud_ref, wide_ref,
 ):
+    own = crm_ref.shape[2]
+
+    def widen(level, carry):
+        q = crm_ref[1, level].astype(F32)
+        m = crm_ref[0, level].astype(F32) + 2.0 * q
+        for f, x in enumerate((m, q)):
+            wide_ref[f, level, PAD : PAD + own] = x
+            wide_ref[f, level, PAD + own + 2 * SUB : PAD + own + 2 * SUB + 1] = x[:1]
+        return carry
+
+    lax.fori_loop(0, crm_ref.shape[1], widen, 0, unroll=UNROLL)
     left_ref[...] = courant_ref[...] * (1.0 / SIDE) + 1.0
     here_ref[...] = (0.7 - courant_ref[...]) * (1.0 / SIDE)
     cloud_ref[...] = mask_ref[...].astype(F32) * 0.3
     peers = map_ref.shape[0]
     targets = map_ref[...]
-    here = (targets >> 7) == place_ref[0]
+    here = (targets >> 7) == lax.axis_index("wide")
     local = (targets & (LANES - 1)).astype(F32) + 1.0
     count = dot(here.astype(BF16), before_matrix(), ((1,), (0,)))
     slots = []
@@ -173,25 +185,33 @@
     return body, (start, start)
 
 
-def start_kernel(place_ref, crm_ref, near_ref, far_ref, left_ref, here_ref, out_ref, load_ref):
-    levels = crm_ref.shape[1]
-    odd = (place_ref[1] & 1) == 1
-
-    def load(level, carry):
-        fields = []
-        for f in range(2):
-            near = near_ref[f, level].astype(F32)
-            far = far_ref[f, level].astype(F32)
-            halo = jnp.where(
-                odd, jnp.concatenate([far, near], axis=0), jnp.concatenate([near, far], axis=0)
-            )
-            fields.append(jnp.concatenate([crm_ref[f, level].astype(F32), halo], axis=0))
-        put(load_ref, 0, level, fields[0] + 2.0 * fields[1])
-        put(load_ref, 1, level, fields[1])
-        return carry
-
-    lax.fori_loop(0, levels, load, 0, unroll=UNROLL)
+def start_kernel(near_ref, far_ref, left_ref, here_ref, wide_ref, out_ref, load_ref):
+    levels = near_ref.shape[1]
     rows = out_ref.shape[2]
+    halo = 2 * SUB
+    odd = (lax.axis_index("narrow") & 1) == 1
+
+    def add_halo(high_ref, low_ref):
+        def load(level, carry):
+            sides = [
+                jnp.concatenate([high_ref[f, level].astype(F32), low_ref[f, level].astype(F32)], axis=0)
+                for f in range(2)
+            ]
+            sides[0] = sides[0] + 2.0 * sides[1]
+            for f in range(2):
+                load_ref[f, level, PAD + rows - halo : PAD + rows] = sides[f]
+                load_ref[f, level, PAD - 1 : PAD] = sides[f][halo - 1 :]
+            return carry
+
+        lax.fori_loop(0, levels, load, 0, unroll=UNROLL)
+
+    @pl.when(odd)
+    def _():
+        add_halo(far_ref, near_ref)
+
+    @pl.when(jnp.logical_not(odd))
+    def _():
+        add_halo(near_ref, far_ref)
 
     def mixed(level):
         left, here = left_ref[pl.ds(level, 1), :], here_ref[pl.ds(level, 1), :]
@@ -332,11 +352,10 @@
 
 
 VM = pl.BlockSpec(memory_space=pltpu.VMEM)
-SM = pl.BlockSpec(memory_space=pltpu.SMEM)
 HB = pl.BlockSpec(memory_space=pltpu.HBM)
 
 
-def call(kernel, shapes, specs, *args, scratch=(), room=4, outs=None):
+def call(kernel, shapes, specs, *args, scratch=(), room=4, outs=None, alias=None):
     out = [jax.ShapeDtypeStruct(s, d) for s, d in shapes]
     many = len(out) > 1
     return pl.pallas_call(
@@ -345,6 +364,7 @@
         in_specs=specs,
         out_specs=outs or ([VM] * len(out) if many else VM),
         scratch_shapes=list(scratch),
+        input_output_aliases=alias or {},
         compiler_params=pltpu.CompilerParams(vmem_limit_bytes=room << 20),
     )(*args)
 
@@ -355,7 +375,6 @@
     columns, width = gcm_state.shape
     levels = crm_state.shape[1]
     own = crm_state.shape[2]
-    place = jnp.stack([lax.axis_index("wide"), lax.axis_index("narrow")]).astype(jnp.int32)
     targets = column_map.reshape(peers, columns)
     n = peers * ROWS
     near = [[g * NEAR + i for i in range(NEAR)] for g in range(ring // NEAR)]
@@ -371,28 +390,28 @@
         [((n, LANES), BF16), ((peers, LANES), BF16), ((8, LANES), jnp.int32)]
         + [((2, levels, SUB, LANES), BF16)] * 2
         + resident[:1] + resident[2:],
-        [SM] + [HB] * 7, place, *[pltpu.with_memory_space_constraint(x, pltpu.HBM) for x in args],
+        [HB] * 7, *[pltpu.with_memory_space_constraint(x, pltpu.HBM) for x in args],
         scratch=[pltpu.VMEM((width, LANES), F32), pltpu.SemaphoreType.DMA((7,))],
     )
     arrived = lax.all_to_all(
         wire.reshape(n // 2, 2, LANES), "wide", split_axis=0, concat_axis=0, tiled=True
     ).reshape(n, LANES)
+    halo_far = lax.ppermute(other, "narrow", other_pairs)
     halo_near = lax.ppermute(face, "narrow", pairs)
-    halo_far = lax.ppermute(other, "narrow", other_pairs)
-
-    slots, take, take_rank, left, here, cloud = call(
+
+    full = own + 2 * SUB
+    padded = full + 2 * PAD
+    slots, take, take_rank, left, here, cloud, widened = call(
         route_kernel,
         [((peers, CAP * LANES), BF16), ((n, 2 * LANES), BF16), ((8, LANES), jnp.int32)]
-        + [((levels, LANES), F32)] * 3,
-        [SM] + [VM] * 3, place, targets, courant, cloud_mask,
-    )
-    full = own + 2 * SUB
-    padded = full + 2 * PAD
-    started = call(
-        start_kernel, [((2, levels, full, LANES), F32)], [SM] + [VM] * 5,
-        place, crm, halo_near, halo_far, left, here,
-        scratch=[pltpu.VMEM((2, levels, padded, LANES), F32)],
-        room=6,
+        + [((levels, LANES), F32)] * 3
+        + [((2, levels, padded, LANES), F32)],
+        [VM] * 4, targets, crm, courant, cloud_mask,
+    )
+    started, _ = call(
+        start_kernel, [((2, levels, full, LANES), F32), ((2, levels, padded, LANES), F32)],
+        [VM] * 5, halo_near, halo_far, left, here, widened,
+        room=6, alias={4: 1},
     )
     crm_new, diff = call(
         main_kernel,
@@ -414,15 +433,15 @@
         diff.reshape(NEAR, rows, LANES), "narrow", split_axis=0, concat_axis=0,
         axis_index_groups=near, tiled=True,
     )
-    back = call(turn_kernel, [((peers, LANES), F32)], [VM] * 2, parts, slots)
+    sums = call(sum_kernel, [((NEAR, rows, LANES), F32)], [VM], parts)
+    sums = lax.all_to_all(
+        sums, "narrow", split_axis=0, concat_axis=0, axis_index_groups=far, tiled=True
+    )
+    back = call(turn_kernel, [((peers, LANES), F32)], [VM] * 2, sums, slots)
     back = lax.all_to_all(
         back.reshape(peers, 1, LANES), "wide", split_axis=0, concat_axis=0, tiled=True
     ).reshape(peers, LANES)
     change = call(back_kernel, [((NEAR, rows, LANES), F32)], [VM] * 3, back, owner, send_rank)
-    change = lax.all_to_all(
-        change, "narrow", split_axis=0, concat_axis=0, axis_index_groups=far, tiled=True
-    )
-    change = call(sum_kernel, [((NEAR, rows, LANES), F32)], [VM], change)
     change = lax.all_to_all(
         change, "narrow", split_axis=0, concat_axis=0, axis_index_groups=near, tiled=True
     )

time: 100 us -> 98.8 us (0.988); the launches traced: 98.4 us -> 98.4 us
  Pallas kernels: 9.76 us -> 8.15 us
  blocking collectives: 54.2 us -> 55.6 us
    all_to_all x2 -> x1, blocking collectives: 25.7 us -> 7.01 us  [shards(): lax.all_to_all(change, 'narrow', split_axis=0, concat_axis=0, axis_index_...]
    all_to_all x0 -> x1, blocking collectives: none -> 18.4 us  [shards(): lax.all_to_all(sums, 'narrow', split_axis=0, concat_axis=0, axis_index_gr...]
    pallas_call x8, Pallas kernels: 9.76 us -> 8.15 us  [call(): pl.pallas_call(kernel, out_shape=out if many else out[0], in_specs=specs,...]
    all_to_all x1, blocking collectives: 21.5 us -> 23.1 us  [shards(): lax.all_to_all(back.reshape(peers, 1, LANES), 'wide', split_axis=0, conca...]
  transfers between devices with their start and end apart: 3 -> 3, of which waited for: 1 -> 1; matrix products, arithmetic and copies ran while one was open for 0% -> 0% of each run, Pallas kernels for 2% -> 1%
where the time goes in v5:
time: 98.8 us; the launch traced here: 98.4 us
  blocking collectives  55.6 us (56%)
  starting transfers between devices  31.7 us (32%)
  Pallas kernels  8.15 us (8%)
  waiting for transfers between devices  2.28 us (2%)
    all_to_all x1, blocking collectives, shards(): lax.all_to_all(back.reshape(peers, 1, LANES), 'wide', split_axis=0, conca...  23.1 us
    all_to_all x1, blocking collectives, shards(): lax.all_to_all(sums, 'narrow', split_axis=0, concat_axis=0, axis_index_gr...  18.4 us
    all_to_all x1, starting transfers between devices, shards(): lax.all_to_all(wire.reshape(n // 2, 2, LANES), 'wide', split_axis=0, conc...  18.2 us
    ppermute x1, starting transfers between devices, shards(): halo_far = lax.ppermute(other, 'narrow', other_pairs)  11.6 us
    pallas_call x8, Pallas kernels, call(): pl.pallas_call(kernel, out_shape=out if many else out[0], in_specs=specs,...  8.15 us
    all_to_all x1, blocking collectives, shards(): lax.all_to_all(diff.reshape(NEAR, rows, LANES), 'narrow', split_axis=0, c...  7.06 us
    all_to_all x1, blocking collectives, shards(): lax.all_to_all(change, 'narrow', split_axis=0, concat_axis=0, axis_index_...  7.01 us
    ppermute x1, waiting for transfers between devices, shards(): halo_far = lax.ppermute(other, 'narrow', other_pairs)  2.27 us
  transfers between devices with their start and end apart: 3, of which 1 were waited for; matrix products, arithmetic and copies ran while one was open for 0% of the time, Pallas kernels for 1%

profile of v5, /device:TPU:1, one launch (start us, length us, event | category | flops | bytes accessed | tf_op | source)
XLA Modules:
  0.0 98.4 jit_solution(17620175200305517461)
XLA Ops:
  0.6 2.0 %shard_map.86 = (bf16[384,128]{1,0:T(8,128)(2,1)}, bf16[64,128]{1,0:T(8,128)(2,1)S(1)}, s32[8,128]{1,0:T(8,128)S(1)}, bf16[2,60,4,128]{3,2,1,0:T(4,128)(2,1)S(1)...) custom-call(s32[64,128]{1,0:T(8,128)} %bitcast.19, ...), custom_call_target="tpu_custom_call" | custom-call | tf_op jit(solution)/shard_map/pallas_call | solution.py:361
  2.7 18.2 %all-to-all-start = ((bf16[192,2,128]{2,1,0:T(2,128)(2,1)}), bf16[192,2,128]{2,1,0:T(2,128)(2,1)S(1)}, u32[]{:S(2)}, u32[]{:S(2)}) async-start(bf16[192,2,128]{2,1,0:T(2,128)(2,1)} %bitcast.3), calls=%async_computation | async-start | bytes 196608 | tf_op jit(solution)/shard_map/all_to_all | solution.py:396
  20.8 1.9 %collective-permute-start = (bf16[2,60,4,128]{3,2,1,0:T(4,128)(2,1)S(1)}, bf16[2,60,4,128]{3,2,1,0:T(4,128)(2,1)S(1)}, u32[]{:S(2)}, u32[]{:S(2)}) collective-permute-start(bf16[2,60,4,128]{3,2,1,0:T(4,128)(2,1)S(1)} %get-tuple-element.30), channel_id=1, source_target_pairs={{0,1},{1,0},{2,3},{3,2},{4,5},{5,4},{6,7},{7,6},{8,9},{9,8},{10,11... | collective-permute-start | bytes 368648 | tf_op jit(solution)/shard_map/ppermute | solution.py:400
  22.8 11.6 %collective-permute-start.1 = (bf16[2,60,4,128]{3,2,1,0:T(4,128)(2,1)S(1)}, bf16[2,60,4,128]{3,2,1,0:T(4,128)(2,1)S(1)}, u32[]{:S(2)}, u32[]{:S(2)}) collective-permute-start(bf16[2,60,4,128]{3,2,1,0:T(4,128)(2,1)S(1)} %get-tuple-element.31), channel_id=1, source_target_pairs={{0,15},{1,2},{2,1},{3,4},{4,3},{5,6},{6,5},{7,8},{8,7},{9,10},{10,... | collective-permute-start | bytes 368648 | tf_op jit(solution)/shard_map/ppermute | solution.py:399
  34.4 0.7 shard_map.87
  35.1 0.0 collective-permute-done.near_ref
  35.1 2.3 %collective-permute-done.1.far_ref = bf16[2,60,4,128]{3,2,1,0:T(4,128)(2,1)S(1)} collective-permute-done((bf16[2,60,4,128]{3,2,1,0:T(4,128)(2,1)S(1)}, bf16[2,60,4,128]{3,2,1,0:T(4,128)(2,1)S(1)}, u32[]{:S(2)}, u32[]{:S(2)}) %collective-permute-start.1) | collective-permute-done | bytes 122912 | tf_op jit(solution)/shard_map/ppermute | solution.py:399
  37.4 0.6 shard_map.88
  38.0 0.0 all-to-all-done
  38.0 3.4 %shard_map.89 = (bf16[2,60,16,128]{3,2,1,0:T(8,128)(2,1)}, f32[2,64,128]{2,1,0:T(8,128)S(1)}) custom-call(bf16[384,128]{1,0:T(8,128)(2,1)S(1)} %bitcast.12, bf16[384,256]{1,0:T(8,128)(2,1)S(1)} %get-tuple-element.28.take_ref, s32[8,128]{1,0:T(8,128)S(1)} %get-tuple-element.29.rank_ref, f32[2,60,24,128]{3,2,1,0:T(8,128)S(1)} %get-tuple-element.35.start_ref, ...), custom_call_target="tpu_custom_call" | custom-call | tf_op jit(solution)/shard_map/pallas_call | solution.py:361
  41.5 7.1 %all_to_all.25.part_ref = f32[4,32,128]{2,1,0:T(8,128)S(1)} all-to-all(f32[4,32,128]{2,1,0:T(8,128)S(1)} %bitcast.16), channel_id=1, replica_groups={{0,1,2,3},{4,5,6,7},{8,9,10,11},{12,13,14,15},{16,17,18,19},{20,21,22,2..., dimensions={0} | all-to-all | bytes 131072 | tf_op jit(solution)/shard_map/all_to_all | solution.py:432
  48.5 18.4 %all_to_all.26.part_ref = f32[4,32,128]{2,1,0:T(8,128)S(1)} all-to-all(f32[4,32,128]{2,1,0:T(8,128)S(1)} %shard_map.90), channel_id=1, replica_groups={{0,4,8,12},{1,5,9,13},{2,6,10,14},{3,7,11,15},{16,20,24,28},{17,21,25,2..., dimensions={0} | all-to-all | bytes 131072 | tf_op jit(solution)/shard_map/all_to_all | solution.py:437
  67.0 0.2 shard_map.91
  67.2 23.1 %all_to_all.27 = f32[64,1,128]{2,1,0:T(1,128)S(1)} all-to-all(f32[64,1,128]{2,1,0:T(1,128)S(1)} %bitcast.14), channel_id=1, replica_groups=mesh['wide'=64,'narrow'=16] {'wide'}, dimensions={0} | all-to-all | bytes 65536 | tf_op jit(solution)/shard_map/all_to_all | solution.py:441
  90.3 0.2 shard_map.92
  90.5 7.0 %all_to_all.28 = f32[4,32,128]{2,1,0:T(8,128)S(1)} all-to-all(f32[4,32,128]{2,1,0:T(8,128)S(1)} %shard_map.92), channel_id=1, replica_groups={{0,1,2,3},{4,5,6,7},{8,9,10,11},{12,13,14,15},{16,17,18,19},{20,21,22,2..., dimensions={0} | all-to-all | bytes 131072 | tf_op jit(solution)/shard_map/all_to_all | solution.py:445
  97.5 0.9 shard_map.93
  (1 shorter events, 0.0 us)
Async XLA Ops:
  2.7 35.3 %all-to-all-start = ((bf16[192,2,128]{2,1,0:T(2,128)(2,1)}), bf16[192,2,128]{2,1,0:T(2,128)(2,1)S(1)}, u32[]{:S(2)}, u32[]{:S(2)}) async-start(bf16[192,2,128]{2,1,0:T(2,128)(2,1)} %bitcast.3), calls=%async_computation | async-start | bytes 196608 | tf_op jit(solution)/shard_map/all_to_all | solution.py:396
  20.8 14.3 %collective-permute-start = (bf16[2,60,4,128]{3,2,1,0:T(4,128)(2,1)S(1)}, bf16[2,60,4,128]{3,2,1,0:T(4,128)(2,1)S(1)}, u32[]{:S(2)}, u32[]{:S(2)}) collective-permute-start(bf16[2,60,4,128]{3,2,1,0:T(4,128)(2,1)S(1)} %get-tuple-element.30), channel_id=1, source_target_pairs={{0,1},{1,0},{2,3},{3,2},{4,5},{5,4},{6,7},{7,6},{8,9},{9,8},{10,11... | collective-permute-start | bytes 368648 | tf_op jit(solution)/shard_map/ppermute | solution.py:400
  22.8 14.6 %collective-permute-start.1 = (bf16[2,60,4,128]{3,2,1,0:T(4,128)(2,1)S(1)}, bf16[2,60,4,128]{3,2,1,0:T(4,128)(2,1)S(1)}, u32[]{:S(2)}, u32[]{:S(2)}) collective-permute-start(bf16[2,60,4,128]{3,2,1,0:T(4,128)(2,1)S(1)} %get-tuple-element.31), channel_id=1, source_target_pairs={{0,15},{1,2},{2,1},{3,4},{4,3},{5,6},{6,5},{7,8},{8,7},{9,10},{10,... | collective-permute-start | bytes 368648 | tf_op jit(solution)/shard_map/ppermute | solution.py:399

commit v6 on v5

--- a/solution.py
+++ b/solution.py
@@ -13,6 +13,7 @@
 LANES = 128
 EXTRA = 16
 NEAR = 4
+HEAD = 36
 SIDE = 0.15
 STEP = 1.0 / (0.1 * SIDE)
 PAD = 8
@@ -42,7 +43,7 @@
 def row_parts(start):
     row = iota((LANES, LANES), 0) + start
     peer = (row * 10923) >> 16
-    return peer, row - peer * ROWS
+    return peer ^ HEAD, row - peer * ROWS
 
 
 def before_matrix():
@@ -65,7 +66,7 @@
     copies[0].wait()
     peers = map_ref.shape[0]
     mine = map_ref[pl.ds(lax.axis_index("wide"), 1), :] >> 7
-    own = iota((peers, LANES), 0) == mine
+    own = (iota((peers, LANES), 0) ^ HEAD) == mine
     own_b = own.astype(BF16)
     count = dot(own_b, before_matrix(), ((1,), (0,)))
     rank = jnp.sum(jnp.where(own, count, 0.0), axis=0, keepdims=True).astype(jnp.int32)
@@ -139,18 +140,20 @@
         hit = here & (count == float(k))
         one = jnp.sum(jnp.where(hit, local, 0.0), axis=1, keepdims=True)
         slots.append((one == lane).astype(F32))
+    swap = ((iota((peers, peers), 0) ^ HEAD) == iota((peers, peers), 1)).astype(BF16)
     rank = jnp.zeros((1, LANES), F32)
     anyslot = jnp.zeros((peers, LANES), F32)
     for k in range(CAP):
         rank = rank + float(k) * jnp.sum(slots[k], axis=0, keepdims=True)
         anyslot = anyslot + slots[k]
-        slot_ref[:, k * LANES : (k + 1) * LANES] = slots[k].astype(BF16)
+        moved = dot(swap, slots[k].astype(BF16), ((1,), (0,)))
+        slot_ref[:, k * LANES : (k + 1) * LANES] = moved.astype(BF16)
     rank_ref[...] = jnp.broadcast_to(rank, rank_ref.shape).astype(jnp.int32)
     n = peers * ROWS
     row = iota((n, peers), 0)
     peer = (row * 10923) >> 16
     part = row - peer * ROWS
-    same = peer == iota((n, peers), 1)
+    same = (peer ^ HEAD) == iota((n, peers), 1)
     main = jnp.zeros((n, LANES), F32)
     for k in range(CAP):
         main = main + dot((same & (part == k)).astype(BF16), slots[k].astype(BF16), ((1,), (0,)))
@@ -377,8 +380,9 @@
     own = crm_state.shape[2]
     targets = column_map.reshape(peers, columns)
     n = peers * ROWS
-    near = [[g * NEAR + i for i in range(NEAR)] for g in range(ring // NEAR)]
-    far = [[g + NEAR * i for i in range(ring // NEAR)] for g in range(NEAR)]
+    wide = [[p ^ HEAD for p in range(peers)]]
+    near = [[g * NEAR + i for i in reversed(range(NEAR))] for g in range(ring // NEAR)]
+    far = [[g + NEAR * i for i in (2, 3, 1, 0)] for g in range(NEAR)]
     pairs = [(i, i ^ 1) for i in range(ring)]
     other_pairs = [(i, ((i + 1) ^ 1) - 1) for i in range(ring)]
     other_pairs = [(a, b % ring) for a, b in other_pairs]
@@ -394,7 +398,8 @@
         scratch=[pltpu.VMEM((width, LANES), F32), pltpu.SemaphoreType.DMA((7,))],
     )
     arrived = lax.all_to_all(
-        wire.reshape(n // 2, 2, LANES), "wide", split_axis=0, concat_axis=0, tiled=True
+        wire.reshape(n // 2, 2, LANES), "wide", split_axis=0, concat_axis=0,
+        axis_index_groups=wide, tiled=True,
     ).reshape(n, LANES)
     halo_far = lax.ppermute(other, "narrow", other_pairs)
     halo_near = lax.ppermute(face, "narrow", pairs)
@@ -439,7 +444,8 @@
     )
     back = call(turn_kernel, [((peers, LANES), F32)], [VM] * 2, sums, slots)
     back = lax.all_to_all(
-        back.reshape(peers, 1, LANES), "wide", split_axis=0, concat_axis=0, tiled=True
+        back.reshape(peers, 1, LANES), "wide", split_axis=0, concat_axis=0,
+        axis_index_groups=wide, tiled=True,
     ).reshape(peers, LANES)
     change = call(back_kernel, [((NEAR, rows, LANES), F32)], [VM] * 3, back, owner, send_rank)
     change = lax.all_to_all(

time: 98.8 us -> 88 us (0.89)
  blocking collectives: 55.6 us -> 42.3 us
  starting transfers between devices: 31.7 us -> 33.8 us
    all_to_all x1, blocking collectives: 23.1 us -> 15.5 us  [shards(): lax.all_to_all(back.reshape(peers, 1, LANES), 'wide', split_axis=0, conca...]
    all_to_all x1, starting transfers between devices: 18.2 us -> 24 us  [shards(): lax.all_to_all(wire.reshape(n // 2, 2, LANES), 'wide', split_axis=0, conc...]
    all_to_all x1, blocking collectives: 18.4 us -> 13.7 us  [shards(): lax.all_to_all(sums, 'narrow', split_axis=0, concat_axis=0, axis_index_gr...]
    ppermute x1, starting transfers between devices: 11.6 us -> 7.86 us  [shards(): halo_far = lax.ppermute(other, 'narrow', other_pairs)]
where the time goes in v6:
time: 88 us; the launch traced here: 87.3 us
  blocking collectives  42.3 us (48%)
  starting transfers between devices  33.8 us (38%)
  Pallas kernels  8.15 us (9%)
  waiting for transfers between devices  2.34 us (3%)
    all_to_all x1, starting transfers between devices, shards(): lax.all_to_all(wire.reshape(n // 2, 2, LANES), 'wide', split_axis=0, conc...  24 us
    all_to_all x1, blocking collectives, shards(): lax.all_to_all(back.reshape(peers, 1, LANES), 'wide', split_axis=0, conca...  15.5 us
    all_to_all x1, blocking collectives, shards(): lax.all_to_all(sums, 'narrow', split_axis=0, concat_axis=0, axis_index_gr...  13.7 us
    pallas_call x8, Pallas kernels, call(): pl.pallas_call(kernel, out_shape=out if many else out[0], in_specs=specs,...  8.15 us
    ppermute x1, starting transfers between devices, shards(): halo_far = lax.ppermute(other, 'narrow', other_pairs)  7.86 us
    all_to_all x1, blocking collectives, shards(): lax.all_to_all(change, 'narrow', split_axis=0, concat_axis=0, axis_index_...  6.76 us
    all_to_all x1, blocking collectives, shards(): lax.all_to_all(diff.reshape(NEAR, rows, LANES), 'narrow', split_axis=0, c...  6.37 us
    ppermute x1, waiting for transfers between devices, shards(): halo_far = lax.ppermute(other, 'narrow', other_pairs)  2.34 us
  transfers between devices with their start and end apart: 3, of which 1 were waited for; matrix products, arithmetic and copies ran while one was open for 0% of the time, Pallas kernels for 1%

profile of v6, /device:TPU:1, one launch (start us, length us, event | category | flops | bytes accessed | tf_op | source)
XLA Modules:
  0.0 87.3 jit_solution(4731410411548344046)
XLA Ops:
  0.6 2.0 %shard_map.86 = (bf16[384,128]{1,0:T(8,128)(2,1)}, bf16[64,128]{1,0:T(8,128)(2,1)S(1)}, s32[8,128]{1,0:T(8,128)S(1)}, bf16[2,60,4,128]{3,2,1,0:T(4,128)(2,1)S(1)...) custom-call(s32[64,128]{1,0:T(8,128)} %bitcast.19, ...), custom_call_target="tpu_custom_call" | custom-call | tf_op jit(solution)/shard_map/pallas_call | solution.py:364
  2.7 24.0 %all-to-all-start = ((bf16[192,2,128]{2,1,0:T(2,128)(2,1)}), bf16[192,2,128]{2,1,0:T(2,128)(2,1)S(1)}, u32[]{:S(2)}, u32[]{:S(2)}) async-start(bf16[192,2,128]{2,1,0:T(2,128)(2,1)} %bitcast.3), calls=%async_computation | async-start | bytes 196608 | tf_op jit(solution)/shard_map/all_to_all | solution.py:400
  26.7 1.9 %collective-permute-start = (bf16[2,60,4,128]{3,2,1,0:T(4,128)(2,1)S(1)}, bf16[2,60,4,128]{3,2,1,0:T(4,128)(2,1)S(1)}, u32[]{:S(2)}, u32[]{:S(2)}) collective-permute-start(bf16[2,60,4,128]{3,2,1,0:T(4,128)(2,1)S(1)} %get-tuple-element.30), channel_id=1, source_target_pairs={{0,1},{1,0},{2,3},{3,2},{4,5},{5,4},{6,7},{7,6},{8,9},{9,8},{10,11... | collective-permute-start | bytes 368648 | tf_op jit(solution)/shard_map/ppermute | solution.py:405
  28.6 7.9 %collective-permute-start.1 = (bf16[2,60,4,128]{3,2,1,0:T(4,128)(2,1)S(1)}, bf16[2,60,4,128]{3,2,1,0:T(4,128)(2,1)S(1)}, u32[]{:S(2)}, u32[]{:S(2)}) collective-permute-start(bf16[2,60,4,128]{3,2,1,0:T(4,128)(2,1)S(1)} %get-tuple-element.31), channel_id=1, source_target_pairs={{0,15},{1,2},{2,1},{3,4},{4,3},{5,6},{6,5},{7,8},{8,7},{9,10},{10,... | collective-permute-start | bytes 368648 | tf_op jit(solution)/shard_map/ppermute | solution.py:404
  36.5 0.7 shard_map.87
  37.2 0.0 collective-permute-done.near_ref
  37.2 2.3 %collective-permute-done.1.far_ref = bf16[2,60,4,128]{3,2,1,0:T(4,128)(2,1)S(1)} collective-permute-done((bf16[2,60,4,128]{3,2,1,0:T(4,128)(2,1)S(1)}, bf16[2,60,4,128]{3,2,1,0:T(4,128)(2,1)S(1)}, u32[]{:S(2)}, u32[]{:S(2)}) %collective-permute-start.1) | collective-permute-done | bytes 122912 | tf_op jit(solution)/shard_map/ppermute | solution.py:404
  39.5 0.6 shard_map.88
  40.1 0.0 all-to-all-done
  40.2 3.4 %shard_map.89 = (bf16[2,60,16,128]{3,2,1,0:T(8,128)(2,1)}, f32[2,64,128]{2,1,0:T(8,128)S(1)}) custom-call(bf16[384,128]{1,0:T(8,128)(2,1)S(1)} %bitcast.12, bf16[384,256]{1,0:T(8,128)(2,1)S(1)} %get-tuple-element.28.take_ref, s32[8,128]{1,0:T(8,128)S(1)} %get-tuple-element.29.rank_ref, f32[2,60,24,128]{3,2,1,0:T(8,128)S(1)} %get-tuple-element.35.start_ref, ...), custom_call_target="tpu_custom_call" | custom-call | tf_op jit(solution)/shard_map/pallas_call | solution.py:364
  43.6 6.4 %all_to_all.25.part_ref = f32[4,32,128]{2,1,0:T(8,128)S(1)} all-to-all(f32[4,32,128]{2,1,0:T(8,128)S(1)} %bitcast.16), channel_id=1, replica_groups={{3,2,1,0},{7,6,5,4},{11,10,9,8},{15,14,13,12},{19,18,17,16},{23,22,21,2..., dimensions={0} | all-to-all | bytes 131072 | tf_op jit(solution)/shard_map/all_to_all | solution.py:437
  50.0 13.7 %all_to_all.26.part_ref = f32[4,32,128]{2,1,0:T(8,128)S(1)} all-to-all(f32[4,32,128]{2,1,0:T(8,128)S(1)} %shard_map.90), channel_id=1, replica_groups={{8,12,4,0},{9,13,5,1},{10,14,6,2},{11,15,7,3},{24,28,20,16},{25,29,21,1..., dimensions={0} | all-to-all | bytes 131072 | tf_op jit(solution)/shard_map/all_to_all | solution.py:442
  63.7 0.2 shard_map.91
  63.9 15.5 %all_to_all.27 = f32[64,1,128]{2,1,0:T(1,128)S(1)} all-to-all(f32[64,1,128]{2,1,0:T(1,128)S(1)} %bitcast.14), channel_id=1, replica_groups={{576,592,608,624,512,528,544,560,704,720,736,752,640,656,672,688,832,84..., dimensions={0} | all-to-all | bytes 65536 | tf_op jit(solution)/shard_map/all_to_all | solution.py:446
  79.4 0.2 shard_map.92
  79.6 6.8 %all_to_all.28 = f32[4,32,128]{2,1,0:T(8,128)S(1)} all-to-all(f32[4,32,128]{2,1,0:T(8,128)S(1)} %shard_map.92), channel_id=1, replica_groups={{3,2,1,0},{7,6,5,4},{11,10,9,8},{15,14,13,12},{19,18,17,16},{23,22,21,2..., dimensions={0} | all-to-all | bytes 131072 | tf_op jit(solution)/shard_map/all_to_all | solution.py:451
  86.4 0.9 %shard_map.93 = bf16[144,128]{1,0:T(8,128)(2,1)} custom-call(f32[128,128]{1,0:T(8,128)S(1)} %bitcast.13, f32[60,72]{1,0:T(8,128)S(1)} %get-tuple-element.42.up_ref), custom_call_target="tpu_custom_call" | custom-call | tf_op jit(solution)/shard_map/pallas_call | solution.py:364
  (1 shorter events, 0.0 us)
Async XLA Ops:
  2.7 37.5 %all-to-all-start = ((bf16[192,2,128]{2,1,0:T(2,128)(2,1)}), bf16[192,2,128]{2,1,0:T(2,128)(2,1)S(1)}, u32[]{:S(2)}, u32[]{:S(2)}) async-start(bf16[192,2,128]{2,1,0:T(2,128)(2,1)} %bitcast.3), calls=%async_computation | async-start | bytes 196608 | tf_op jit(solution)/shard_map/all_to_all | solution.py:400
  26.7 10.5 %collective-permute-start = (bf16[2,60,4,128]{3,2,1,0:T(4,128)(2,1)S(1)}, bf16[2,60,4,128]{3,2,1,0:T(4,128)(2,1)S(1)}, u32[]{:S(2)}, u32[]{:S(2)}) collective-permute-start(bf16[2,60,4,128]{3,2,1,0:T(4,128)(2,1)S(1)} %get-tuple-element.30), channel_id=1, source_target_pairs={{0,1},{1,0},{2,3},{3,2},{4,5},{5,4},{6,7},{7,6},{8,9},{9,8},{10,11... | collective-permute-start | bytes 368648 | tf_op jit(solution)/shard_map/ppermute | solution.py:405
  28.6 10.9 %collective-permute-start.1 = (bf16[2,60,4,128]{3,2,1,0:T(4,128)(2,1)S(1)}, bf16[2,60,4,128]{3,2,1,0:T(4,128)(2,1)S(1)}, u32[]{:S(2)}, u32[]{:S(2)}) collective-permute-start(bf16[2,60,4,128]{3,2,1,0:T(4,128)(2,1)S(1)} %get-tuple-element.31), channel_id=1, source_target_pairs={{0,15},{1,2},{2,1},{3,4},{4,3},{5,6},{6,5},{7,8},{8,7},{9,10},{10,... | collective-permute-start | bytes 368648 | tf_op jit(solution)/shard_map/ppermute | solution.py:404

commit v7 on v6

--- a/solution.py
+++ b/solution.py
@@ -52,9 +52,9 @@
 
 def pack_kernel(
     map_hbm, state_hbm, crm_hbm, courant_hbm, mask_hbm, down_hbm, up_hbm,
-    wire_ref, owner_ref, rank_ref, face_ref, other_ref,
+    wire_hbm, owner_ref, rank_ref, face_ref, other_ref,
     map_ref, crm_ref, courant_ref, mask_ref, down_ref, up_ref,
-    state_ref, sems,
+    state_ref, wire_ref, sems, out_sems,
 ):
     pairs = (
         (map_hbm, map_ref), (state_hbm, state_ref), (crm_hbm, crm_ref), (courant_hbm, courant_ref),
@@ -85,7 +85,13 @@
         main = (to_peer & (part == rank)).astype(BF16)
         tail = (to_peer & (part == CAP)).astype(BF16)
         wire = dot(main, state[:LANES], ((1,), (1,))) + dot(tail, spread, ((1,), (1,)))
-        wire_ref[start : start + LANES] = wire.astype(BF16)
+        rows = pl.ds(start, LANES)
+        wire_ref[rows] = wire.astype(BF16)
+        out = pltpu.make_async_copy(
+            wire_ref.at[rows], wire_hbm.at[rows], out_sems.at[start // LANES]
+        )
+        out.start()
+        copies.append(out)
     copies[2].wait()
     own_columns = crm_ref.shape[2]
     odd = (lax.axis_index("narrow") & 1) == 1
@@ -343,15 +349,22 @@
     out_ref[...] = jnp.broadcast_to(jnp.sum(part_ref[...], axis=0)[None], out_ref.shape)
 
 
-def end_kernel(change_ref, up_ref, out_ref):
+def end_kernel(change_ref, up_ref, out_hbm, out_ref, sems):
     levels, gcm = up_ref.shape
     half = change_ref.shape[0] // 2
+    copies = []
     for f in range(2):
         tend = lax.dot_general(
             up_ref[...], change_ref[f * half : f * half + levels], (((0,), (0,)), ((), ())),
             precision=HI, preferred_element_type=F32,
         ) * (1.0 / (CX * SUB))
-        out_ref[f * gcm : (f + 1) * gcm] = tend.astype(BF16)
+        rows = pl.ds(f * gcm, gcm)
+        out_ref[f] = tend.astype(BF16)
+        copy = pltpu.make_async_copy(out_ref.at[f], out_hbm.at[rows], sems.at[f])
+        copy.start()
+        copies.append(copy)
+    for copy in copies:
+        copy.wait()
 
 
 VM = pl.BlockSpec(memory_space=pltpu.VMEM)
@@ -395,7 +408,13 @@
         + [((2, levels, SUB, LANES), BF16)] * 2
         + resident[:1] + resident[2:],
         [HB] * 7, *[pltpu.with_memory_space_constraint(x, pltpu.HBM) for x in args],
-        scratch=[pltpu.VMEM((width, LANES), F32), pltpu.SemaphoreType.DMA((7,))],
+        scratch=[
+            pltpu.VMEM((width, LANES), F32),
+            pltpu.VMEM((n, LANES), BF16),
+            pltpu.SemaphoreType.DMA((7,)),
+            pltpu.SemaphoreType.DMA((n // LANES,)),
+        ],
+        outs=[HB] + [VM] * 10,
     )
     arrived = lax.all_to_all(
         wire.reshape(n // 2, 2, LANES), "wide", split_axis=0, concat_axis=0,
@@ -452,7 +471,9 @@
         change, "narrow", split_axis=0, concat_axis=0, axis_index_groups=near, tiled=True
     )
     tendency = call(
-        end_kernel, [((width, LANES), BF16)], [VM] * 2, change.reshape(NEAR * rows, LANES), up
+        end_kernel, [((width, LANES), BF16)], [VM] * 2, change.reshape(NEAR * rows, LANES), up,
+        scratch=[pltpu.VMEM((2, width // 2, LANES), BF16), pltpu.SemaphoreType.DMA((2,))],
+        outs=HB,
     )
     return tendency.T, crm_new
 

time: 88 us -> 87.9 us (level)
  no operation moved by 1% of the time
where the time goes in v7:
time: 87.9 us; the launch traced here: 87.2 us
  blocking collectives  42.3 us (48%)
  starting transfers between devices  33.8 us (38%)
  Pallas kernels  8 us (9%)
  waiting for transfers between devices  2.34 us (3%)
    all_to_all x1, starting transfers between devices, shards(): lax.all_to_all(wire.reshape(n // 2, 2, LANES), 'wide', split_axis=0, conc...  24 us
    all_to_all x1, blocking collectives, shards(): lax.all_to_all(back.reshape(peers, 1, LANES), 'wide', split_axis=0, conca...  15.5 us
    all_to_all x1, blocking collectives, shards(): lax.all_to_all(sums, 'narrow', split_axis=0, concat_axis=0, axis_index_gr...  13.7 us
    pallas_call x8, Pallas kernels, call(): pl.pallas_call(kernel, out_shape=out if many else out[0], in_specs=specs,...  8 us
    ppermute x1, starting transfers between devices, shards(): halo_far = lax.ppermute(other, 'narrow', other_pairs)  7.86 us
    all_to_all x1, blocking collectives, shards(): lax.all_to_all(change, 'narrow', split_axis=0, concat_axis=0, axis_index_...  6.76 us
    all_to_all x1, blocking collectives, shards(): lax.all_to_all(diff.reshape(NEAR, rows, LANES), 'narrow', split_axis=0, c...  6.37 us
    ppermute x1, waiting for transfers between devices, shards(): halo_far = lax.ppermute(other, 'narrow', other_pairs)  2.34 us
  transfers between devices with their start and end apart: 3, of which 1 were waited for; matrix products, arithmetic and copies ran while one was open for 0% of the time, Pallas kernels for 1%

profile of v7, /device:TPU:1, one launch (start us, length us, event | category | flops | bytes accessed | tf_op | source)
XLA Modules:
  0.0 87.2 jit_solution(1851890696801512244)
XLA Ops:
  0.6 1.8 %shard_map.86 = (bf16[384,128]{1,0:T(8,128)(2,1)}, bf16[64,128]{1,0:T(8,128)(2,1)S(1)}, s32[8,128]{1,0:T(8,128)S(1)}, bf16[2,60,4,128]{3,2,1,0:T(4,128)(2,1)S(1)...) custom-call(s32[64,128]{1,0:T(8,128)} %bitcast.19, ...), custom_call_target="tpu_custom_call" | custom-call | tf_op jit(solution)/shard_map/pallas_call | solution.py:377
  2.5 24.0 %all-to-all-start = ((bf16[192,2,128]{2,1,0:T(2,128)(2,1)}), bf16[192,2,128]{2,1,0:T(2,128)(2,1)S(1)}, u32[]{:S(2)}, u32[]{:S(2)}) async-start(bf16[192,2,128]{2,1,0:T(2,128)(2,1)} %bitcast.3), calls=%async_computation | async-start | bytes 196608 | tf_op jit(solution)/shard_map/all_to_all | solution.py:419
  26.5 1.9 %collective-permute-start = (bf16[2,60,4,128]{3,2,1,0:T(4,128)(2,1)S(1)}, bf16[2,60,4,128]{3,2,1,0:T(4,128)(2,1)S(1)}, u32[]{:S(2)}, u32[]{:S(2)}) collective-permute-start(bf16[2,60,4,128]{3,2,1,0:T(4,128)(2,1)S(1)} %get-tuple-element.30), channel_id=1, source_target_pairs={{0,1},{1,0},{2,3},{3,2},{4,5},{5,4},{6,7},{7,6},{8,9},{9,8},{10,11... | collective-permute-start | bytes 368648 | tf_op jit(solution)/shard_map/ppermute | solution.py:424
  28.5 7.9 %collective-permute-start.1 = (bf16[2,60,4,128]{3,2,1,0:T(4,128)(2,1)S(1)}, bf16[2,60,4,128]{3,2,1,0:T(4,128)(2,1)S(1)}, u32[]{:S(2)}, u32[]{:S(2)}) collective-permute-start(bf16[2,60,4,128]{3,2,1,0:T(4,128)(2,1)S(1)} %get-tuple-element.31), channel_id=1, source_target_pairs={{0,15},{1,2},{2,1},{3,4},{4,3},{5,6},{6,5},{7,8},{8,7},{9,10},{10,... | collective-permute-start | bytes 368648 | tf_op jit(solution)/shard_map/ppermute | solution.py:423
  36.3 0.7 shard_map.87
  37.0 0.0 collective-permute-done.near_ref
  37.0 2.3 %collective-permute-done.1.far_ref = bf16[2,60,4,128]{3,2,1,0:T(4,128)(2,1)S(1)} collective-permute-done((bf16[2,60,4,128]{3,2,1,0:T(4,128)(2,1)S(1)}, bf16[2,60,4,128]{3,2,1,0:T(4,128)(2,1)S(1)}, u32[]{:S(2)}, u32[]{:S(2)}) %collective-permute-start.1) | collective-permute-done | bytes 122912 | tf_op jit(solution)/shard_map/ppermute | solution.py:423
  39.3 0.6 shard_map.88
  40.0 0.0 all-to-all-done
  40.0 3.4 %shard_map.89 = (bf16[2,60,16,128]{3,2,1,0:T(8,128)(2,1)}, f32[2,64,128]{2,1,0:T(8,128)S(1)}) custom-call(bf16[384,128]{1,0:T(8,128)(2,1)S(1)} %bitcast.12, bf16[384,256]{1,0:T(8,128)(2,1)S(1)} %get-tuple-element.28.take_ref, s32[8,128]{1,0:T(8,128)S(1)} %get-tuple-element.29.rank_ref, f32[2,60,24,128]{3,2,1,0:T(8,128)S(1)} %get-tuple-element.35.start_ref, ...), custom_call_target="tpu_custom_call" | custom-call | tf_op jit(solution)/shard_map/pallas_call | solution.py:377
  43.4 6.4 %all_to_all.25.part_ref = f32[4,32,128]{2,1,0:T(8,128)S(1)} all-to-all(f32[4,32,128]{2,1,0:T(8,128)S(1)} %bitcast.16), channel_id=1, replica_groups={{3,2,1,0},{7,6,5,4},{11,10,9,8},{15,14,13,12},{19,18,17,16},{23,22,21,2..., dimensions={0} | all-to-all | bytes 131072 | tf_op jit(solution)/shard_map/all_to_all | solution.py:456
  49.8 13.7 %all_to_all.26.part_ref = f32[4,32,128]{2,1,0:T(8,128)S(1)} all-to-all(f32[4,32,128]{2,1,0:T(8,128)S(1)} %shard_map.90), channel_id=1, replica_groups={{8,12,4,0},{9,13,5,1},{10,14,6,2},{11,15,7,3},{24,28,20,16},{25,29,21,1..., dimensions={0} | all-to-all | bytes 131072 | tf_op jit(solution)/shard_map/all_to_all | solution.py:461
  63.5 0.2 shard_map.91
  63.7 15.5 %all_to_all.27 = f32[64,1,128]{2,1,0:T(1,128)S(1)} all-to-all(f32[64,1,128]{2,1,0:T(1,128)S(1)} %bitcast.14), channel_id=1, replica_groups={{576,592,608,624,512,528,544,560,704,720,736,752,640,656,672,688,832,84..., dimensions={0} | all-to-all | bytes 65536 | tf_op jit(solution)/shard_map/all_to_all | solution.py:465
  79.2 0.2 shard_map.92
  79.4 6.8 %all_to_all.28 = f32[4,32,128]{2,1,0:T(8,128)S(1)} all-to-all(f32[4,32,128]{2,1,0:T(8,128)S(1)} %shard_map.92), channel_id=1, replica_groups={{3,2,1,0},{7,6,5,4},{11,10,9,8},{15,14,13,12},{19,18,17,16},{23,22,21,2..., dimensions={0} | all-to-all | bytes 131072 | tf_op jit(solution)/shard_map/all_to_all | solution.py:470
  86.2 1.0 %shard_map.93 = bf16[144,128]{1,0:T(8,128)(2,1)} custom-call(f32[128,128]{1,0:T(8,128)S(1)} %bitcast.13, f32[60,72]{1,0:T(8,128)S(1)} %get-tuple-element.42.up_ref), custom_call_target="tpu_custom_call" | custom-call | tf_op jit(solution)/shard_map/pallas_call | solution.py:377
  (1 shorter events, 0.0 us)
Async XLA Ops:
  2.5 37.5 %all-to-all-start = ((bf16[192,2,128]{2,1,0:T(2,128)(2,1)}), bf16[192,2,128]{2,1,0:T(2,128)(2,1)S(1)}, u32[]{:S(2)}, u32[]{:S(2)}) async-start(bf16[192,2,128]{2,1,0:T(2,128)(2,1)} %bitcast.3), calls=%async_computation | async-start | bytes 196608 | tf_op jit(solution)/shard_map/all_to_all | solution.py:419
  26.5 10.5 %collective-permute-start = (bf16[2,60,4,128]{3,2,1,0:T(4,128)(2,1)S(1)}, bf16[2,60,4,128]{3,2,1,0:T(4,128)(2,1)S(1)}, u32[]{:S(2)}, u32[]{:S(2)}) collective-permute-start(bf16[2,60,4,128]{3,2,1,0:T(4,128)(2,1)S(1)} %get-tuple-element.30), channel_id=1, source_target_pairs={{0,1},{1,0},{2,3},{3,2},{4,5},{5,4},{6,7},{7,6},{8,9},{9,8},{10,11... | collective-permute-start | bytes 368648 | tf_op jit(solution)/shard_map/ppermute | solution.py:424
  28.5 10.9 %collective-permute-start.1 = (bf16[2,60,4,128]{3,2,1,0:T(4,128)(2,1)S(1)}, bf16[2,60,4,128]{3,2,1,0:T(4,128)(2,1)S(1)}, u32[]{:S(2)}, u32[]{:S(2)}) collective-permute-start(bf16[2,60,4,128]{3,2,1,0:T(4,128)(2,1)S(1)} %get-tuple-element.31), channel_id=1, source_target_pairs={{0,15},{1,2},{2,1},{3,4},{4,3},{5,6},{6,5},{7,8},{8,7},{9,10},{10,... | collective-permute-start | bytes 368648 | tf_op jit(solution)/shard_map/ppermute | solution.py:423

commit v8 on v7

--- a/solution.py
+++ b/solution.py
@@ -18,7 +18,7 @@
 STEP = 1.0 / (0.1 * SIDE)
 PAD = 8
 PIECES = 3
-UNROLL = 5
+UNROLL = 10
 HI = lax.Precision.HIGHEST
 F32 = jnp.float32
 BF16 = jnp.bfloat16
@@ -259,7 +259,9 @@
     for index in range(SUB):
         for f in range(2):
             force_ref[index, f, :levels] = (0.25 * STEP ** (index + 1)) * force[f]
-    diff_ref[:, levels:] = jnp.zeros((2, diff_ref.shape[1] - levels, LANES), F32)
+    diff_ref[...] = jnp.zeros_like(diff_ref)
+    half = diff_ref.shape[0] // 2
+    flip = jnp.where(lax.axis_index("narrow") < NEAR, diff_ref.shape[0] * 3 // NEAR, 0)
 
     def physics(pair, level, index):
         m = pair[0] + force_ref[index, 0, pl.ds(level, 1), :]
@@ -296,7 +298,8 @@
             for f, x in enumerate((t, q)):
                 new_ref[f, level] = x.astype(BF16)
                 change = x - crm_ref[f, level].astype(F32)
-                diff_ref[f, pl.ds(level, 1), :] = jnp.sum(change, axis=0, keepdims=True)
+                row = (f * half + level) ^ flip
+                diff_ref[pl.ds(row, 1), :] = jnp.sum(change, axis=0, keepdims=True)
 
         body, carry = column(levels, mixed, keep)
         if not last:
@@ -439,7 +442,7 @@
     )
     crm_new, diff = call(
         main_kernel,
-        [((2, levels, own, LANES), BF16), ((2, ring * 4, LANES), F32)],
+        [((2, levels, own, LANES), BF16), ((2 * ring * 4, LANES), F32)],
         [VM] * 9,
         arrived, take, take_rank, started, crm, left, here, cloud, down,
         scratch=[
@@ -455,7 +458,7 @@
     rows = 2 * ring * 4 // NEAR
     parts = lax.all_to_all(
         diff.reshape(NEAR, rows, LANES), "narrow", split_axis=0, concat_axis=0,
-        axis_index_groups=near, tiled=True,
+        axis_index_groups=[near[0][::-1], *near[1:]], tiled=True,
     )
     sums = call(sum_kernel, [((NEAR, rows, LANES), F32)], [VM], parts)
     sums = lax.all_to_all(

time: 87.9 us -> 88.1 us (level)
  no operation moved by 1% of the time
where the time goes in v8:
time: 88.1 us; the launch traced here: 87.4 us
  blocking collectives  42.8 us (49%)
  starting transfers between devices  33.8 us (38%)
  Pallas kernels  7.67 us (9%)
  waiting for transfers between devices  2.36 us (3%)
    all_to_all x1, starting transfers between devices, shards(): lax.all_to_all(wire.reshape(n // 2, 2, LANES), 'wide', split_axis=0, conc...  24 us
    all_to_all x1, blocking collectives, shards(): lax.all_to_all(back.reshape(peers, 1, LANES), 'wide', split_axis=0, conca...  15.1 us
    all_to_all x1, blocking collectives, shards(): lax.all_to_all(sums, 'narrow', split_axis=0, concat_axis=0, axis_index_gr...  14.4 us
    ppermute x1, starting transfers between devices, shards(): halo_far = lax.ppermute(other, 'narrow', other_pairs)  7.86 us
    pallas_call x8, Pallas kernels, call(): pl.pallas_call(kernel, out_shape=out if many else out[0], in_specs=specs,...  7.67 us
    all_to_all x1, blocking collectives, shards(): lax.all_to_all(diff.reshape(NEAR, rows, LANES), 'narrow', split_axis=0, c...  7.04 us
    all_to_all x1, blocking collectives, shards(): lax.all_to_all(change, 'narrow', split_axis=0, concat_axis=0, axis_index_...  6.37 us
    ppermute x1, waiting for transfers between devices, shards(): halo_far = lax.ppermute(other, 'narrow', other_pairs)  2.36 us
  transfers between devices with their start and end apart: 3, of which 1 were waited for; matrix products, arithmetic and copies ran while one was open for 0% of the time, Pallas kernels for 1%

profile of v8, /device:TPU:1, one launch (start us, length us, event | category | flops | bytes accessed | tf_op | source)
XLA Modules:
  0.0 87.4 jit_solution(1902605928687306422)
XLA Ops:
  0.6 1.8 %shard_map.86 = (bf16[384,128]{1,0:T(8,128)(2,1)}, bf16[64,128]{1,0:T(8,128)(2,1)S(1)}, s32[8,128]{1,0:T(8,128)S(1)}, bf16[2,60,4,128]{3,2,1,0:T(4,128)(2,1)S(1)...) custom-call(s32[64,128]{1,0:T(8,128)} %bitcast.19, ...), custom_call_target="tpu_custom_call" | custom-call | tf_op jit(solution)/shard_map/pallas_call | solution.py:380
  2.5 24.0 %all-to-all-start = ((bf16[192,2,128]{2,1,0:T(2,128)(2,1)}), bf16[192,2,128]{2,1,0:T(2,128)(2,1)S(1)}, u32[]{:S(2)}, u32[]{:S(2)}) async-start(bf16[192,2,128]{2,1,0:T(2,128)(2,1)} %bitcast.3), calls=%async_computation | async-start | bytes 196608 | tf_op jit(solution)/shard_map/all_to_all | solution.py:422
  26.5 1.9 %collective-permute-start = (bf16[2,60,4,128]{3,2,1,0:T(4,128)(2,1)S(1)}, bf16[2,60,4,128]{3,2,1,0:T(4,128)(2,1)S(1)}, u32[]{:S(2)}, u32[]{:S(2)}) collective-permute-start(bf16[2,60,4,128]{3,2,1,0:T(4,128)(2,1)S(1)} %get-tuple-element.30), channel_id=1, source_target_pairs={{0,1},{1,0},{2,3},{3,2},{4,5},{5,4},{6,7},{7,6},{8,9},{9,8},{10,11... | collective-permute-start | bytes 368648 | tf_op jit(solution)/shard_map/ppermute | solution.py:427
  28.5 7.9 %collective-permute-start.1 = (bf16[2,60,4,128]{3,2,1,0:T(4,128)(2,1)S(1)}, bf16[2,60,4,128]{3,2,1,0:T(4,128)(2,1)S(1)}, u32[]{:S(2)}, u32[]{:S(2)}) collective-permute-start(bf16[2,60,4,128]{3,2,1,0:T(4,128)(2,1)S(1)} %get-tuple-element.31), channel_id=1, source_target_pairs={{0,15},{1,2},{2,1},{3,4},{4,3},{5,6},{6,5},{7,8},{8,7},{9,10},{10,... | collective-permute-start | bytes 368648 | tf_op jit(solution)/shard_map/ppermute | solution.py:426
  36.3 0.6 shard_map.87
  37.0 0.0 collective-permute-done.near_ref
  37.0 2.4 %collective-permute-done.1.far_ref = bf16[2,60,4,128]{3,2,1,0:T(4,128)(2,1)S(1)} collective-permute-done((bf16[2,60,4,128]{3,2,1,0:T(4,128)(2,1)S(1)}, bf16[2,60,4,128]{3,2,1,0:T(4,128)(2,1)S(1)}, u32[]{:S(2)}, u32[]{:S(2)}) %collective-permute-start.1) | collective-permute-done | bytes 122912 | tf_op jit(solution)/shard_map/ppermute | solution.py:426
  39.3 0.6 shard_map.88
  39.9 0.0 all-to-all-done
  39.9 3.2 %shard_map.89 = (bf16[2,60,16,128]{3,2,1,0:T(8,128)(2,1)}, f32[128,128]{1,0:T(8,128)S(1)}) custom-call(bf16[384,128]{1,0:T(8,128)(2,1)S(1)} %bitcast.12, bf16[384,256]{1,0:T(8,128)(2,1)S(1)} %get-tuple-element.28.take_ref, s32[8,128]{1,0:T(8,128)S(1)} %get-tuple-element.29.rank_ref, f32[2,60,24,128]{3,2,1,0:T(8,128)S(1)} %get-tuple-element.35.start_ref, ...), custom_call_target="tpu_custom_call" | custom-call | tf_op jit(solution)/shard_map/pallas_call | solution.py:380
  43.1 7.0 %all_to_all.25.part_ref = f32[4,32,128]{2,1,0:T(8,128)S(1)} all-to-all(f32[4,32,128]{2,1,0:T(8,128)S(1)} %bitcast.16), channel_id=1, replica_groups={{0,1,2,3},{7,6,5,4},{11,10,9,8},{15,14,13,12},{16,17,18,19},{23,22,21,2..., dimensions={0} | all-to-all | bytes 131072 | tf_op jit(solution)/shard_map/all_to_all | solution.py:459
  50.2 14.4 %all_to_all.26.part_ref = f32[4,32,128]{2,1,0:T(8,128)S(1)} all-to-all(f32[4,32,128]{2,1,0:T(8,128)S(1)} %shard_map.90), channel_id=1, replica_groups={{8,12,4,0},{9,13,5,1},{10,14,6,2},{11,15,7,3},{24,28,20,16},{25,29,21,1..., dimensions={0} | all-to-all | bytes 131072 | tf_op jit(solution)/shard_map/all_to_all | solution.py:464
  64.6 0.2 shard_map.91
  64.8 15.1 %all_to_all.27 = f32[64,1,128]{2,1,0:T(1,128)S(1)} all-to-all(f32[64,1,128]{2,1,0:T(1,128)S(1)} %bitcast.14), channel_id=1, replica_groups={{576,592,608,624,512,528,544,560,704,720,736,752,640,656,672,688,832,84..., dimensions={0} | all-to-all | bytes 65536 | tf_op jit(solution)/shard_map/all_to_all | solution.py:468
  79.9 0.2 shard_map.92
  80.1 6.4 %all_to_all.28 = f32[4,32,128]{2,1,0:T(8,128)S(1)} all-to-all(f32[4,32,128]{2,1,0:T(8,128)S(1)} %shard_map.92), channel_id=1, replica_groups={{3,2,1,0},{7,6,5,4},{11,10,9,8},{15,14,13,12},{19,18,17,16},{23,22,21,2..., dimensions={0} | all-to-all | bytes 131072 | tf_op jit(solution)/shard_map/all_to_all | solution.py:473
  86.5 1.0 %shard_map.93 = bf16[144,128]{1,0:T(8,128)(2,1)} custom-call(f32[128,128]{1,0:T(8,128)S(1)} %bitcast.13, f32[60,72]{1,0:T(8,128)S(1)} %get-tuple-element.42.up_ref), custom_call_target="tpu_custom_call" | custom-call | tf_op jit(solution)/shard_map/pallas_call | solution.py:380
  (1 shorter events, 0.0 us)
Async XLA Ops:
  2.5 37.4 %all-to-all-start = ((bf16[192,2,128]{2,1,0:T(2,128)(2,1)}), bf16[192,2,128]{2,1,0:T(2,128)(2,1)S(1)}, u32[]{:S(2)}, u32[]{:S(2)}) async-start(bf16[192,2,128]{2,1,0:T(2,128)(2,1)} %bitcast.3), calls=%async_computation | async-start | bytes 196608 | tf_op jit(solution)/shard_map/all_to_all | solution.py:422
  26.5 10.4 %collective-permute-start = (bf16[2,60,4,128]{3,2,1,0:T(4,128)(2,1)S(1)}, bf16[2,60,4,128]{3,2,1,0:T(4,128)(2,1)S(1)}, u32[]{:S(2)}, u32[]{:S(2)}) collective-permute-start(bf16[2,60,4,128]{3,2,1,0:T(4,128)(2,1)S(1)} %get-tuple-element.30), channel_id=1, source_target_pairs={{0,1},{1,0},{2,3},{3,2},{4,5},{5,4},{6,7},{7,6},{8,9},{9,8},{10,11... | collective-permute-start | bytes 368648 | tf_op jit(solution)/shard_map/ppermute | solution.py:427
  28.5 10.9 %collective-permute-start.1 = (bf16[2,60,4,128]{3,2,1,0:T(4,128)(2,1)S(1)}, bf16[2,60,4,128]{3,2,1,0:T(4,128)(2,1)S(1)}, u32[]{:S(2)}, u32[]{:S(2)}) collective-permute-start(bf16[2,60,4,128]{3,2,1,0:T(4,128)(2,1)S(1)} %get-tuple-element.31), channel_id=1, source_target_pairs={{0,15},{1,2},{2,1},{3,4},{4,3},{5,6},{6,5},{7,8},{8,7},{9,10},{10,... | collective-permute-start | bytes 368648 | tf_op jit(solution)/shard_map/ppermute | solution.py:426
